TPU v7x, 256 devices: a whole 4x4x8 slice. The times are simulated.
256 devices in a mesh: dp: 4 (over x), ctx: 8 (over z), tp: 8 (over y, core).
Axes of the slice: x: 4, y: 4, z: 8, core: 2. Of those that a mesh axis runs over, the one named last changes fastest.
Arguments:
- query: bfloat16 [4096, 8192], P(('dp', 'ctx'), 'tp'), may hold values from -6 to 6
- key_in: bfloat16 [4096, 8192], P(('dp', 'ctx'), 'tp'), may hold values from -6 to 6
- value_in: bfloat16 [4096, 8192], P(('dp', 'ctx'), 'tp'), may hold values from -6 to 6
- gate: bfloat16 [4096, 8192], P(('dp', 'ctx'), 'tp'), may hold values from -6 to 6
- out_grad: bfloat16 [4096, 8192], P(('dp', 'ctx')), may hold values from -6 to 6
- proj_weight: bfloat16 [8192, 8192], P('tp', ('dp', 'ctx')), may hold values from -0.0625 to 0.0625
- mr_filter: bfloat16 [512, 128], P('tp'), may hold values from -0.5 to 0.5
- lr_rate: float32 [512, 16], P('tp'), may hold values from 1.953125e-05 to 0.05
- lr_residue: float32 [512, 16], P('tp'), may hold values from -0.6 to 0.6
Outputs:
- query_grad: bfloat16 [4096, 8192], P(('dp', 'ctx'), 'tp')
- conv_grad: bfloat16 [4096, 8192], P(('dp', 'ctx'), 'tp')
- gate_grad: bfloat16 [4096, 8192], P(('dp', 'ctx'), 'tp')
- weight_grad_t: bfloat16 [8192, 8192], P(('dp', 'ctx'), 'tp')
All inputs are finite; a program needn't handle non-finite values.
Results may differ from a plain program's by a relative error of at most 0.028.
Values may be sent and summed in bfloat16 or wider, within the bound.
A program may use at most 128 MiB of HBM per device.

v0:
```python
import jax
import jax.numpy as jnp
from jax import lax
from jax.sharding import PartitionSpec as P

GROUP = 16
MR_TAPS = 128
ORDER = 16


HIGHEST = lax.Precision.HIGHEST


def shifted(value, axis, steps):
    count = lax.axis_size(axis)
    leading, last = (max(0, -steps), min(count, count - steps))
    return lax.ppermute(value, axis, [(source, source + steps) for source in range(leading, last)])


def mr_matrix(filters, row_count, taps):
    out_pos = jnp.arange(row_count)[:, None]
    in_pos = jnp.arange(row_count + taps)[None, :]
    lag_index = taps + out_pos - in_pos
    valid = (lag_index >= 0) & (lag_index < taps)
    picked = jnp.take(filters, jnp.clip(lag_index, 0, taps - 1), axis=1)
    return jnp.where(valid[None], picked, jnp.zeros_like(picked))


def lr_tables(rates, residues, row_count):
    counts = jnp.arange(row_count + 1).astype(jnp.float32)
    powers = jnp.exp(-rates[None, :, :] * counts[:, None, None])
    kernel = jnp.sum(residues[None] * powers[:row_count], axis=2)
    lag_index = jnp.arange(row_count)[:, None] - jnp.arange(row_count)[None, :]
    picked = jnp.take(kernel.T, jnp.clip(lag_index, 0, row_count - 1), axis=1)
    toeplitz = jnp.where((lag_index >= 0)[None], picked, jnp.zeros_like(picked))
    carry_coef = (residues[None] * powers[1:]).transpose(1, 0, 2)
    end_coef = powers[:row_count][::-1].transpose(1, 2, 0)
    start_coef = powers[:row_count].transpose(1, 2, 0)
    back_coef = (residues[None] * powers[1:][::-1]).transpose(1, 0, 2)
    block_decay = powers[row_count].T
    return (toeplitz, carry_coef, end_coef, start_coef, back_coef, block_decay)


def lanes_last(array, row_count, groups):
    return array.reshape(row_count, groups, GROUP).transpose(1, 2, 0)


def rows_first(array, row_count, local_width):
    return array.transpose(2, 0, 1).reshape(row_count, local_width)


def on_device(query, key_in, value_in, gate, out_grad, proj_weight, mr_filter, lr_rate, lr_residue):
    row_count, local_width = query.shape
    groups = local_width // GROUP
    product = (key_in.astype(jnp.float32) * value_in.astype(jnp.float32)).astype(jnp.bfloat16)
    conv_rim = shifted(product, "ctx", 1)
    extended = jnp.concatenate([conv_rim, product], axis=0).reshape(
        row_count + MR_TAPS, groups, GROUP
    )
    conv_matrix = mr_matrix(mr_filter, row_count, MR_TAPS)
    conv_out = jnp.einsum(
        "gtu,ugi->tgi", conv_matrix, extended, preferred_element_type=jnp.float32
    ).reshape(row_count, local_width)
    mixed = (query.astype(jnp.float32) * conv_out).astype(jnp.bfloat16)
    toeplitz, carry_coef, end_coef, start_coef, back_coef, block_decay = lr_tables(
        lr_rate, lr_residue, row_count
    )
    decay_full = jnp.repeat(block_decay, GROUP, axis=1)
    mixed_lanes = lanes_last(mixed.astype(jnp.float32), row_count, groups)
    local_part = jnp.einsum("gtv,giv->git", toeplitz, mixed_lanes, precision=HIGHEST)
    ends = jnp.einsum("gnt,git->ngi", end_coef, mixed_lanes, precision=HIGHEST).reshape(
        ORDER, local_width
    )

    def pass_forward(step, received):
        return shifted((decay_full * received + ends).astype(jnp.bfloat16), "ctx", 1).astype(
            jnp.float32
        )

    incoming = lax.fori_loop(0, lax.axis_size("ctx") - 1, pass_forward, jnp.zeros_like(ends))
    carried = jnp.einsum(
        "gtn,ngi->git", carry_coef, incoming.reshape(ORDER, groups, GROUP), precision=HIGHEST
    )
    long_out = rows_first(local_part + carried, row_count, local_width)
    gated = (gate.astype(jnp.float32) * long_out).astype(jnp.bfloat16)
    columns = out_grad
    out_delta = lax.dot_general(
        columns,
        lax.all_gather(proj_weight, ("dp", "ctx"), axis=1, tiled=True),
        (((1,), (1,)), ((), ())),
        preferred_element_type=jnp.float32,
    )
    seed_lanes = lanes_last(out_delta * gate.astype(jnp.float32), row_count, groups)
    local_back = jnp.einsum("gtv,git->giv", toeplitz, seed_lanes, precision=HIGHEST)
    starts = jnp.einsum("gnt,git->ngi", start_coef, seed_lanes, precision=HIGHEST).reshape(
        ORDER, local_width
    )

    def pass_backward(step, received):
        return shifted((decay_full * received + starts).astype(jnp.bfloat16), "ctx", -1).astype(
            jnp.float32
        )

    later = lax.fori_loop(0, lax.axis_size("ctx") - 1, pass_backward, jnp.zeros_like(starts))
    carried_back = jnp.einsum(
        "gtn,ngi->git", back_coef, later.reshape(ORDER, groups, GROUP), precision=HIGHEST
    )
    mixed_delta = rows_first(local_back + carried_back, row_count, local_width)
    query_grad = (mixed_delta * conv_out).astype(jnp.bfloat16)
    conv_grad = (mixed_delta * query.astype(jnp.float32)).astype(jnp.bfloat16)
    gate_grad = (out_delta * long_out).astype(jnp.bfloat16)
    columns = out_grad
    weight_sum = lax.psum_scatter(
        lax.dot_general(
            columns, gated, (((0,), (0,)), ((), ())), preferred_element_type=jnp.float32
        ).astype(jnp.bfloat16),
        ("dp", "ctx"),
        scatter_dimension=0,
        tiled=True,
    )
    return (query_grad, conv_grad, gate_grad, weight_sum)


def solution(mesh):
    return jax.shard_map(
        on_device,
        mesh=mesh,
        in_specs=(
            P(("dp", "ctx"), "tp"),
            P(("dp", "ctx"), "tp"),
            P(("dp", "ctx"), "tp"),
            P(("dp", "ctx"), "tp"),
            P(("dp", "ctx"), None),
            P("tp", ("dp", "ctx")),
            P("tp", None),
            P("tp", None),
            P("tp", None),
        ),
        out_specs=(
            P(("dp", "ctx"), "tp"),
            P(("dp", "ctx"), "tp"),
            P(("dp", "ctx"), "tp"),
            P(("dp", "ctx"), "tp"),
        ),
        check_vma=False,
    )
```

profile of v0, /device:TPU:8, one launch (start us, length us, event | category | flops | bytes accessed | tf_op | source)
XLA Modules:
  0.0 557.8 jit_solution(4031628447269069721)
XLA Ops:
  9.1 4.5 collective-permute-start.2
  21.3 124.6 %gather_fusion.1 = bf16[32768,64]{1,0:T(8,128)(2,1)} fusion(bf16[64,128]{0,1:T(8,128)(2,1)S(1)} %copy.60, s32[32768]{0:T(1024)} %broadcast_clamp_fusion), kind=kCustom, calls=%fused_computation.1 | custom fusion | bytes 8519680 | tf_op jit(solution)/shard_map/jit(_take)/gather | solution.py:25
  145.9 10.2 %copy.61 = bf16[128,256,64]{1,0,2:T(8,128)(2,1)} copy(bf16[128,256,64]{2,1,0:T(8,128)(2,1)} %bitcast.79) | data formatting | bytes 8388608 | tf_op jit(solution)/shard_map/jit(_take)/gather | solution.py:25
  156.4 54.4 %gather_fusion = f32[16384,64]{1,0:T(8,128)} fusion(f32[64,128]{0,1:T(8,128)S(1)} %bitcast.78, s32[16384]{0:T(1024)S(1)} %copy-done.13), kind=kCustom, calls=%fused_computation | custom fusion | bytes 8454144 | tf_op jit(solution)/shard_map/jit(_take)/gather | solution.py:34
  210.8 7.4 %copy.55 = f32[128,128,64]{1,0,2:T(8,128)} copy(f32[128,128,64]{2,1,0:T(8,128)} %bitcast.80) | data formatting | bytes 8388608 | tf_op jit(solution)/shard_map/jit(_take)/gather | solution.py:34
  228.9 45.9 %while.23 = (s32[]{:T(128)}, f32[16,1024]{1,0:T(8,128)S(1)}, f32[16,1024]{1,0:T(8,128)S(1)}, f32[16,64]{1,0:T(8,128)S(1)}, s32[]{:T(128)}, /*index=5*/s32[]{:T(128)}) while((s32[]{:T(128)}, f32[16,1024]{1,0:T(8,128)S(1)}, f32[16,1024]{1,0:T(8,128)S(1)}, f32[16,64]{1,0:T(8,128)S(1)}, s32[]{:T(128)}, /*index=5*/s32[]{:T(128)}) %tuple.68), condition=%wide.region_4.5_spmd.clone, body=%wide.region_3.4_spmd.clone.sunk | while | flops 81923 | bytes 659575 | solution.py:80
  241.0 4.7 collective-permute-start.1
  247.7 4.2 collective-permute-start.1
  254.0 4.2 collective-permute-start.1
  260.4 5.3 collective-permute-start.1
  267.9 5.4 collective-permute-start.1
  275.8 5.2 fusion.10
  284.8 9.2 %convert_bitcast_fusion = bf16[8192,1024]{0,1:T(8,128)(2,1)} fusion(bf16[128,8192]{1,0:T(8,128)(2,1)S(1)} %copy-done, f32[128,1024]{1,0:T(8,128)} %copy.65, bf16[128,1024]{1,0:T(8,128)(2,1)} %param.16), kind=kOutput, calls=%fused_computation.10 | convolution fusion | flops 2156265472 | bytes 19660800 | tf_op jit(solution)/shard_map/dot_general | solution.py:114
  296.1 12.4 %multiply_convert_fusion = (bf16[128,1024]{1,0:T(8,128)(2,1)}, f32[128,1024]{1,0:T(8,128)}) fusion(f32[128,1024]{1,0:T(8,128)} %copy.65, bf16[128,1024]{1,0:T(8,128)(2,1)} %param.16, bf16[128,8192]{1,0:T(8,128)(2,1)S(1)} %copy-done, bf16[1024,8192]{1,0:T(8,128)(2,1)} %all-gather.2.cloned.1.call-done), kind=kOutput, calls=%fused_computation.52 | convolution fusion | flops 2148007936 | bytes 20447232 | tf_op jit(solution)/shard_map/dot_general | solution.py:87
  314.6 56.8 %while.22 = (s32[]{:T(128)}, f32[16,1024]{1,0:T(8,128)S(1)}, f32[16,1024]{1,0:T(8,128)S(1)}, f32[16,64]{1,0:T(8,128)S(1)}, s32[]{:T(128)}, /*index=5*/s32[]{:T(128)}) while((s32[]{:T(128)}, f32[16,1024]{1,0:T(8,128)S(1)}, f32[16,1024]{1,0:T(8,128)S(1)}, f32[16,64]{1,0:T(8,128)S(1)}, s32[]{:T(128)}, /*index=5*/s32[]{:T(128)}) %tuple.69), condition=%wide.region_2.3_spmd.clone, body=%wide.region_1.2_spmd.clone.sunk | while | flops 81923 | bytes 659575 | solution.py:104
  316.4 6.6 %collective-permute-done = bf16[16,1024]{1,0:T(8,128)(2,1)S(1)} collective-permute-done((bf16[16,1024]{1,0:T(8,128)(2,1)S(1)}, bf16[16,1024]{1,0:T(8,128)(2,1)S(1)}, u32[]{:S(2)}, u32[]{:S(2)}) %collective-permute-start) | collective-permute-done | bytes 32800 | tf_op jit(solution)/shard_map/while/body/eval_jaxpr/ppermute | solution.py:17
  324.8 6.7 %collective-permute-done = bf16[16,1024]{1,0:T(8,128)(2,1)S(1)} collective-permute-done((bf16[16,1024]{1,0:T(8,128)(2,1)S(1)}, bf16[16,1024]{1,0:T(8,128)(2,1)S(1)}, u32[]{:S(2)}, u32[]{:S(2)}) %collective-permute-start) | collective-permute-done | bytes 32800 | tf_op jit(solution)/shard_map/while/body/eval_jaxpr/ppermute | solution.py:17
  333.2 6.2 %collective-permute-done = bf16[16,1024]{1,0:T(8,128)(2,1)S(1)} collective-permute-done((bf16[16,1024]{1,0:T(8,128)(2,1)S(1)}, bf16[16,1024]{1,0:T(8,128)(2,1)S(1)}, u32[]{:S(2)}, u32[]{:S(2)}) %collective-permute-start) | collective-permute-done | bytes 32800 | tf_op jit(solution)/shard_map/while/body/eval_jaxpr/ppermute | solution.py:17
  341.2 6.6 %collective-permute-done = bf16[16,1024]{1,0:T(8,128)(2,1)S(1)} collective-permute-done((bf16[16,1024]{1,0:T(8,128)(2,1)S(1)}, bf16[16,1024]{1,0:T(8,128)(2,1)S(1)}, u32[]{:S(2)}, u32[]{:S(2)}) %collective-permute-start) | collective-permute-done | bytes 32800 | tf_op jit(solution)/shard_map/while/body/eval_jaxpr/ppermute | solution.py:17
  349.6 6.2 %collective-permute-done = bf16[16,1024]{1,0:T(8,128)(2,1)S(1)} collective-permute-done((bf16[16,1024]{1,0:T(8,128)(2,1)S(1)}, bf16[16,1024]{1,0:T(8,128)(2,1)S(1)}, u32[]{:S(2)}, u32[]{:S(2)}) %collective-permute-start) | collective-permute-done | bytes 32800 | tf_op jit(solution)/shard_map/while/body/eval_jaxpr/ppermute | solution.py:17
  357.6 5.8 %collective-permute-done = bf16[16,1024]{1,0:T(8,128)(2,1)S(1)} collective-permute-done((bf16[16,1024]{1,0:T(8,128)(2,1)S(1)}, bf16[16,1024]{1,0:T(8,128)(2,1)S(1)}, u32[]{:S(2)}, u32[]{:S(2)}) %collective-permute-start) | collective-permute-done | bytes 32800 | tf_op jit(solution)/shard_map/while/body/eval_jaxpr/ppermute | solution.py:17
  365.2 6.1 %collective-permute-done = bf16[16,1024]{1,0:T(8,128)(2,1)S(1)} collective-permute-done((bf16[16,1024]{1,0:T(8,128)(2,1)S(1)}, bf16[16,1024]{1,0:T(8,128)(2,1)S(1)}, u32[]{:S(2)}, u32[]{:S(2)}) %collective-permute-start) | collective-permute-done | bytes 32800 | tf_op jit(solution)/shard_map/while/body/eval_jaxpr/ppermute | solution.py:17
  374.4 5.6 %fusion.28 = f32[64,16,128]{2,1,0:T(8,128)S(1)} fusion(f32[64,16,128]{2,1,0:T(8,128)S(1)} %fusion.38, f32[64,16,128]{2,1,0:T(8,128)S(1)} %bitcast.82, f32[128,128,64]{1,0,2:T(8,128)} %copy.55, pred[128,128]{1,0:T(8,128)(4,1)S(1)} %copy-done.16, pred[128,128]{1,0:T(8,128)(4,1)S(1)} %copy-done.18), kind=kOutput, calls=%fused_computation.32 | convolution fusion | flops 203554816 | bytes 5799936 | tf_op jit(solution)/shard_map/gtv,git->giv/dot_general | solution.py:94
  381.8 167.1 %reduce-scatter.2.cloned.1.call-done = bf16[256,1024]{0,1:T(8,128)(2,1)} async-done(((bf16[8192,1024]{0,1:T(8,128)(2,1)}), bf16[256,1024]{0,1:T(8,128)(2,1)}) %reduce-scatter.2.cloned.1.call-update) | async-done | bytes 524304 | tf_op jit(solution)/shard_map/reduce_scatter | solution.py:113
  (166 shorter events, 74.3 us)
Async XLA Ops:
  7.2 277.6 %copy-start = (bf16[128,8192]{1,0:T(8,128)(2,1)S(1)}, bf16[128,8192]{1,0:T(8,128)(2,1)}, u32[]{:S(2)}) copy-start(bf16[128,8192]{1,0:T(8,128)(2,1)} %param.17) | copy-start | bytes 6291460
  7.2 288.9 %all-gather.2.cloned.1.call-start = ((), (), s32[]{:S(2)}) async-start(), calls=%async_computation.1 | async-start | bytes 17301504 | tf_op jit(solution)/shard_map/all_gather | solution.py:89
  7.9 541.0 %reduce-scatter.2.cloned.1.call-start = ((), (), s32[]{:S(2)}) async-start(), calls=%async_computation.2 | async-start | bytes 17301504 | tf_op jit(solution)/shard_map/reduce_scatter | solution.py:113
  9.1 211.6 %collective-permute-start.2 = (bf16[128,1024]{1,0:T(8,128)(2,1)S(1)}, bf16[128,1024]{1,0:T(8,128)(2,1)}, u32[]{:S(2)}, u32[]{:S(2)}) collective-permute-start(bf16[128,1024]{1,0:T(8,128)(2,1)S(1)} %multiply_convert_fusion.1), channel_id=1, source_target_pairs={{0,8},{8,16},{16,24},{24,32},{32,40},{40,48},{48,56},{1,9},{9,17},... | collective-permute-start | bytes 786440 | tf_op jit(solution)/shard_map/ppermute | solution.py:17
  16.9 129.0 %copy-start.1 = (f32[129,64,16]{0,2,1:T(8,128)}, f32[129,64,16]{0,2,1:T(8,128)S(1)}, u32[]{:S(2)}) copy-start(f32[129,64,16]{0,2,1:T(8,128)S(1)} %multiply_exponential_fusion) | copy-start | bytes 1585156
  156.3 70.0 %copy-start.4 = (bf16[128,1024]{0,1:T(8,128)(2,1)}, bf16[128,1024]{0,1:T(8,128)(2,1)S(1)}, u32[]{:S(2)}) copy-start(bf16[128,1024]{0,1:T(8,128)(2,1)S(1)} %copy.62) | copy-start | bytes 786436
  229.4 4.7 collective-permute-start.1
  234.7 5.8 %collective-permute-start.1 = (bf16[16,1024]{1,0:T(8,128)(2,1)S(1)}, bf16[16,1024]{1,0:T(8,128)(2,1)S(1)}, u32[]{:S(2)}, u32[]{:S(2)}) collective-permute-start(bf16[16,1024]{1,0:T(8,128)(2,1)S(1)} %fusion.82), channel_id=1, source_target_pairs={{0,8},{8,16},{16,24},{24,32},{32,40},{40,48},{48,56},{1,9},{9,17},... | collective-permute-start | bytes 98312 | tf_op jit(solution)/shard_map/while/body/eval_jaxpr/ppermute | solution.py:17
  241.0 6.3 %collective-permute-start.1 = (bf16[16,1024]{1,0:T(8,128)(2,1)S(1)}, bf16[16,1024]{1,0:T(8,128)(2,1)S(1)}, u32[]{:S(2)}, u32[]{:S(2)}) collective-permute-start(bf16[16,1024]{1,0:T(8,128)(2,1)S(1)} %fusion.82), channel_id=1, source_target_pairs={{0,8},{8,16},{16,24},{24,32},{32,40},{40,48},{48,56},{1,9},{9,17},... | collective-permute-start | bytes 98312 | tf_op jit(solution)/shard_map/while/body/eval_jaxpr/ppermute | solution.py:17
  247.7 5.8 %collective-permute-start.1 = (bf16[16,1024]{1,0:T(8,128)(2,1)S(1)}, bf16[16,1024]{1,0:T(8,128)(2,1)S(1)}, u32[]{:S(2)}, u32[]{:S(2)}) collective-permute-start(bf16[16,1024]{1,0:T(8,128)(2,1)S(1)} %fusion.82), channel_id=1, source_target_pairs={{0,8},{8,16},{16,24},{24,32},{32,40},{40,48},{48,56},{1,9},{9,17},... | collective-permute-start | bytes 98312 | tf_op jit(solution)/shard_map/while/body/eval_jaxpr/ppermute | solution.py:17
  254.0 5.8 %collective-permute-start.1 = (bf16[16,1024]{1,0:T(8,128)(2,1)S(1)}, bf16[16,1024]{1,0:T(8,128)(2,1)S(1)}, u32[]{:S(2)}, u32[]{:S(2)}) collective-permute-start(bf16[16,1024]{1,0:T(8,128)(2,1)S(1)} %fusion.82), channel_id=1, source_target_pairs={{0,8},{8,16},{16,24},{24,32},{32,40},{40,48},{48,56},{1,9},{9,17},... | collective-permute-start | bytes 98312 | tf_op jit(solution)/shard_map/while/body/eval_jaxpr/ppermute | solution.py:17
  260.4 7.0 %collective-permute-start.1 = (bf16[16,1024]{1,0:T(8,128)(2,1)S(1)}, bf16[16,1024]{1,0:T(8,128)(2,1)S(1)}, u32[]{:S(2)}, u32[]{:S(2)}) collective-permute-start(bf16[16,1024]{1,0:T(8,128)(2,1)S(1)} %fusion.82), channel_id=1, source_target_pairs={{0,8},{8,16},{16,24},{24,32},{32,40},{40,48},{48,56},{1,9},{9,17},... | collective-permute-start | bytes 98312 | tf_op jit(solution)/shard_map/while/body/eval_jaxpr/ppermute | solution.py:17
  267.9 6.9 %collective-permute-start.1 = (bf16[16,1024]{1,0:T(8,128)(2,1)S(1)}, bf16[16,1024]{1,0:T(8,128)(2,1)S(1)}, u32[]{:S(2)}, u32[]{:S(2)}) collective-permute-start(bf16[16,1024]{1,0:T(8,128)(2,1)S(1)} %fusion.82), channel_id=1, source_target_pairs={{0,8},{8,16},{16,24},{24,32},{32,40},{40,48},{48,56},{1,9},{9,17},... | collective-permute-start | bytes 98312 | tf_op jit(solution)/shard_map/while/body/eval_jaxpr/ppermute | solution.py:17
  313.3 59.1 %copy-start.12 = (f32[64,16]{1,0:T(8,128)S(1)}, f32[64,16]{1,0:T(8,128)}, u32[]{:S(2)}) copy-start(f32[64,16]{1,0:T(8,128)} %copy-done.10) | copy-start | bytes 12292
  314.6 59.8 %copy-start.3 = (f32[128,1024]{0,1:T(8,128)S(1)}, f32[128,1024]{0,1:T(8,128)}, u32[]{:S(2)}) copy-start(f32[128,1024]{0,1:T(8,128)} %copy.51) | copy-start | bytes 1572868
  314.6 59.8 %copy-start.16 = (pred[128,128]{1,0:T(8,128)(4,1)S(1)}, pred[128,128]{1,0:T(8,128)(4,1)}, u32[]{:S(2)}) copy-start(pred[128,128]{1,0:T(8,128)(4,1)} %get-tuple-element.147) | copy-start | bytes 49156
  314.6 59.8 %copy-start.18 = (pred[128,128]{1,0:T(8,128)(4,1)S(1)}, pred[128,128]{1,0:T(8,128)(4,1)}, u32[]{:S(2)}) copy-start(pred[128,128]{1,0:T(8,128)(4,1)} %get-tuple-element.148) | copy-start | bytes 49156
  315.1 7.9 %collective-permute-start = (bf16[16,1024]{1,0:T(8,128)(2,1)S(1)}, bf16[16,1024]{1,0:T(8,128)(2,1)S(1)}, u32[]{:S(2)}, u32[]{:S(2)}) collective-permute-start(bf16[16,1024]{1,0:T(8,128)(2,1)S(1)} %fusion.81), channel_id=1, source_target_pairs={{8,0},{16,8},{24,16},{32,24},{40,32},{48,40},{56,48},{9,1},{17,9},... | collective-permute-start | bytes 98312 | tf_op jit(solution)/shard_map/while/body/eval_jaxpr/ppermute | solution.py:17
  323.5 8.0 %collective-permute-start = (bf16[16,1024]{1,0:T(8,128)(2,1)S(1)}, bf16[16,1024]{1,0:T(8,128)(2,1)S(1)}, u32[]{:S(2)}, u32[]{:S(2)}) collective-permute-start(bf16[16,1024]{1,0:T(8,128)(2,1)S(1)} %fusion.81), channel_id=1, source_target_pairs={{8,0},{16,8},{24,16},{32,24},{40,32},{48,40},{56,48},{9,1},{17,9},... | collective-permute-start | bytes 98312 | tf_op jit(solution)/shard_map/while/body/eval_jaxpr/ppermute | solution.py:17
  331.9 7.5 %collective-permute-start = (bf16[16,1024]{1,0:T(8,128)(2,1)S(1)}, bf16[16,1024]{1,0:T(8,128)(2,1)S(1)}, u32[]{:S(2)}, u32[]{:S(2)}) collective-permute-start(bf16[16,1024]{1,0:T(8,128)(2,1)S(1)} %fusion.81), channel_id=1, source_target_pairs={{8,0},{16,8},{24,16},{32,24},{40,32},{48,40},{56,48},{9,1},{17,9},... | collective-permute-start | bytes 98312 | tf_op jit(solution)/shard_map/while/body/eval_jaxpr/ppermute | solution.py:17
  339.9 7.9 %collective-permute-start = (bf16[16,1024]{1,0:T(8,128)(2,1)S(1)}, bf16[16,1024]{1,0:T(8,128)(2,1)S(1)}, u32[]{:S(2)}, u32[]{:S(2)}) collective-permute-start(bf16[16,1024]{1,0:T(8,128)(2,1)S(1)} %fusion.81), channel_id=1, source_target_pairs={{8,0},{16,8},{24,16},{32,24},{40,32},{48,40},{56,48},{9,1},{17,9},... | collective-permute-start | bytes 98312 | tf_op jit(solution)/shard_map/while/body/eval_jaxpr/ppermute | solution.py:17
  348.3 7.5 %collective-permute-start = (bf16[16,1024]{1,0:T(8,128)(2,1)S(1)}, bf16[16,1024]{1,0:T(8,128)(2,1)S(1)}, u32[]{:S(2)}, u32[]{:S(2)}) collective-permute-start(bf16[16,1024]{1,0:T(8,128)(2,1)S(1)} %fusion.81), channel_id=1, source_target_pairs={{8,0},{16,8},{24,16},{32,24},{40,32},{48,40},{56,48},{9,1},{17,9},... | collective-permute-start | bytes 98312 | tf_op jit(solution)/shard_map/while/body/eval_jaxpr/ppermute | solution.py:17
  356.3 7.1 %collective-permute-start = (bf16[16,1024]{1,0:T(8,128)(2,1)S(1)}, bf16[16,1024]{1,0:T(8,128)(2,1)S(1)}, u32[]{:S(2)}, u32[]{:S(2)}) collective-permute-start(bf16[16,1024]{1,0:T(8,128)(2,1)S(1)} %fusion.81), channel_id=1, source_target_pairs={{8,0},{16,8},{24,16},{32,24},{40,32},{48,40},{56,48},{9,1},{17,9},... | collective-permute-start | bytes 98312 | tf_op jit(solution)/shard_map/while/body/eval_jaxpr/ppermute | solution.py:17
  363.9 7.4 %collective-permute-start = (bf16[16,1024]{1,0:T(8,128)(2,1)S(1)}, bf16[16,1024]{1,0:T(8,128)(2,1)S(1)}, u32[]{:S(2)}, u32[]{:S(2)}) collective-permute-start(bf16[16,1024]{1,0:T(8,128)(2,1)S(1)} %fusion.81), channel_id=1, source_target_pairs={{8,0},{16,8},{24,16},{32,24},{40,32},{48,40},{56,48},{9,1},{17,9},... | collective-permute-start | bytes 98312 | tf_op jit(solution)/shard_map/while/body/eval_jaxpr/ppermute | solution.py:17
  (17 other events, 205.4 us)
Sparse Core Ops, SparseCore 0:
  10.5 153.4 all-gather.1
  294.1 254.7 reduce-scatter.1
where the time goes:
time: 561 us; the launch traced here: 558 us
  local copies, waits for them, and re-layouts  223 us (40%)
  waiting for transfers between devices  223 us (40%)
  starting transfers between devices  44.8 us (8%)
  matrix products  43.7 us (8%)
  between operations  14.3 us (3%)
  other arithmetic  8.61 us (2%)
    reduce_scatter x1, waiting for transfers between devices, on_device(): lax.psum_scatter(lax.dot_general(columns, gated, (((0,), (0,)), ((), ()))...  167 us
    gather x2, local copies, waits for them, and re-layouts, mr_matrix(): picked = jnp.take(filters, jnp.clip(lag_index, 0, taps - 1), axis=1)  135 us
    gather x2, local copies, waits for them, and re-layouts, lr_tables(): picked = jnp.take(kernel.T, jnp.clip(lag_index, 0, row_count - 1), axis=1)  61.8 us
    ppermute x15, waiting for transfers between devices, shifted(): lax.ppermute(value, axis, [(source, source + steps) for source in range(l...  55.3 us
    ppermute x15, starting transfers between devices, shifted(): lax.ppermute(value, axis, [(source, source + steps) for source in range(l...  44.8 us
    dot_general x1, matrix products, on_device(): lax.dot_general(columns, lax.all_gather(proj_weight, ('dp', 'ctx'), axis=...  12.4 us
  transfers between devices with their start and end apart: 17, of which 15 were waited for; matrix products, arithmetic and copies ran while one was open for 49% of the time, Pallas kernels for 0%

commit v1 on v0

v1 whole, which is shorter than its diff:
```python
import jax
import jax.numpy as jnp
from jax import lax
from jax.experimental import pallas as pl
from jax.experimental.pallas import tpu as pltpu
from jax.sharding import PartitionSpec as P

GROUP = 16
ORDER = 16
ROWS = 128
WIDTH = 1024
LANES = 128
BLOCKS = WIDTH // LANES
N_DP = 4
N_CTX = 8
N_Y = 4
FEATS = 256
HALF = WIDTH // 2

MESH = pl.DeviceIdType.MESH
HIGHEST = lax.Precision.HIGHEST
BF16 = jnp.bfloat16
F32 = jnp.float32


def remote(src, dst, send, recv, **device):
    return pltpu.make_async_remote_copy(
        src_ref=src, dst_ref=dst, send_sem=send, recv_sem=recv, device_id=device, device_id_type=MESH
    )


def iota(dim, shape=(ROWS, LANES)):
    return lax.broadcasted_iota(jnp.int32, shape, dim)


def skew(row):
    return pltpu.roll(jnp.broadcast_to(row, (ROWS, LANES)), 0, 1, stride=1, stride_axis=0)


def dot(a, b, a_dim=1, b_dim=0, precision=None):
    return lax.dot_general(
        a, b, (((a_dim,), (b_dim,)), ((), ())), precision=precision, preferred_element_type=F32
    )


def own_groups(stacked):
    lane_group = iota(1) // GROUP
    total = jnp.zeros((ROWS, LANES), F32)
    for g in range(LANES // GROUP):
        total = jnp.where(lane_group == g, stacked[g * ROWS : (g + 1) * ROWS], total)
    return total


def fold_modes(modes):
    own = jnp.where(iota(0) // ORDER == iota(1) // GROUP, modes, 0.0)
    total = own[:ORDER]
    for g in range(1, LANES // GROUP):
        total = total + own[g * ORDER : (g + 1) * ORDER]
    return total


def split(value):
    high = value.astype(BF16)
    return high, (value - high.astype(F32)).astype(BF16)


def modal(coef, state):
    spread = jnp.where(
        iota(0) // ORDER == iota(1) // GROUP, jnp.concatenate([state] * (LANES // GROUP), axis=0), 0.0
    )
    coef_high, coef_low = split(coef)
    state_high, state_low = split(spread)
    return dot(coef_high, state_high) + dot(coef_high, state_low) + dot(coef_low, state_high)


def kernel(
    q_ref, k_ref, v_ref, g_ref, og_ref, w_ref, f_ref, rate_ref, res_ref,
    qg_ref, cg_ref, gg_ref, wt_ref,
    prod, halo, og, wg, mr, tf, tb, base, coef_a, coef_e, carry, back, decay,
    conv, mixed, long_out, part, ends, ends_all, starts, starts_all, state,
    rs_out, rs_in, gall, delta, ogt, x1_out, x1_in, x2_out, x2_in,
    a2_send, a2_recv, loc, halo_sem, w_send, w_recv, y_send, y_recv, sib_send, sib_recv,
    st_send, st_recv, rs_send, rs_recv, ag_send, ag_recv, x_send, x_recv,
):
    d, c, t = lax.axis_index("dp"), lax.axis_index("ctx"), lax.axis_index("tp")
    y, core = t // 2, t % 2

    def ctx(step):
        return lax.rem(c + step + N_CTX, N_CTX)

    def dp(step):
        return lax.rem(d + step + N_DP, N_DP)

    def tp(step, side):
        return lax.rem(y + step + N_Y, N_Y) * 2 + side

    sibling = tp(0, 1 - core)

    barrier = pltpu.get_barrier_semaphore()
    for s in range(1, N_CTX):
        pl.semaphore_signal(barrier, inc=1, device_id={"ctx": ctx(s)}, device_id_type=MESH)
    for s in (-1, 1):
        pl.semaphore_signal(barrier, inc=1, device_id={"dp": dp(s)}, device_id_type=MESH)
        pl.semaphore_signal(barrier, inc=1, device_id={"tp": tp(s, core)}, device_id_type=MESH)
    pl.semaphore_signal(barrier, inc=1, device_id={"tp": sibling}, device_id_type=MESH)
    prod[...] = (k_ref[...].astype(F32) * v_ref[...].astype(F32)).astype(BF16)
    pl.semaphore_wait(barrier, N_CTX - 1 + 5)

    def strip(owner):
        return pl.ds(pl.multiple_of(owner * 16, 16), 16)

    def feature_copy(j, s):
        to = ctx(s)
        return remote(
            og_ref.at[strip(t), pl.ds(pl.multiple_of((j * N_CTX + to) * FEATS, FEATS), FEATS)],
            og.at[c, strip(t), pl.ds(j * FEATS, FEATS)],
            a2_send.at[s, j], a2_recv.at[c, j], ctx=to,
        )

    def feature_wait(j, s):
        source = ctx(s)
        remote(
            og_ref.at[strip(t), pl.ds(j * FEATS, FEATS)], og.at[source, strip(t), pl.ds(j * FEATS, FEATS)],
            a2_send.at[s, j], a2_recv.at[source, j], ctx=source,
        ).wait_recv()

    def feature_own(j):
        return pltpu.make_async_copy(
            og_ref.at[strip(t), pl.ds(pl.multiple_of((j * N_CTX + c) * FEATS, FEATS), FEATS)],
            og.at[c, strip(t), pl.ds(j * FEATS, FEATS)], loc.at[j],
        )

    for s in (4, 3, 5, 2, 6, 1, 7):
        for j in range(N_DP):
            feature_copy(j, s).start()
    halo_copy = remote(prod, halo, halo_sem.at[0], halo_sem.at[1], ctx=ctx(1))
    halo_copy.start()
    for j in range(N_DP):
        feature_own(j).start()
    w_own = pltpu.make_async_copy(w_ref, wg.at[d], loc.at[N_DP])
    w_own.start()
    steps = (1, -1)
    for way in range(2):
        remote(w_ref, wg.at[d], w_send.at[way, 0], w_recv.at[way, 0], dp=dp(steps[way])).start()

    reverse = ((iota(0) + iota(1)) % LANES == 0).astype(BF16)
    base[...] = dot(f_ref[...], reverse)
    group_of_lane = iota(1, (8, LANES)) // GROUP
    own_lane = group_of_lane == iota(0, (8, LANES))
    repeat_modes = (iota(1, (ORDER, LANES)) % ORDER == iota(0, (ORDER, LANES))).astype(F32)
    to_channels = (iota(0) // ORDER == iota(1) // GROUP).astype(F32)
    row_at = iota(0).astype(F32)

    def build(b, carried):
        rows8 = pl.ds(pl.multiple_of(b * 8, 8), 8)
        rates = jnp.where(own_lane, dot(rate_ref[rows8, :], repeat_modes, precision=HIGHEST), 0.0)
        weights = jnp.where(own_lane, dot(res_ref[rows8, :], repeat_modes, precision=HIGHEST), 0.0)
        rate = jnp.sum(rates, axis=0, keepdims=True)
        weight = jnp.sum(weights, axis=0, keepdims=True)
        falling = jnp.exp(-rate * row_at)
        rising = jnp.exp(-rate * (ROWS - 1.0 - row_at))
        once = jnp.exp(-rate)
        coef_a[b] = falling.astype(BF16)
        coef_e[b] = rising.astype(BF16)
        carry[b] = weight * once * falling
        back[b] = weight * once * rising
        per_mode = jnp.where(
            iota(1, (ORDER, LANES)) % ORDER == iota(0, (ORDER, LANES)), rate, 0.0
        )
        decay[b] = jnp.exp(-ROWS * dot(per_mode, to_channels, precision=HIGHEST))
        ahead = dot(weights, falling, b_dim=1, precision=HIGHEST)
        behind = dot(
            weights, jnp.where(iota(0) == 0, 1.0, once * rising), b_dim=1, precision=HIGHEST
        )
        taps = base[rows8, :]
        lower = iota(0) >= iota(1)
        upper = iota(1) >= iota(0)
        for g in range(8):
            here = pl.ds(g * ROWS, ROWS)
            taps_at = skew(taps[g : g + 1])
            mr[b, here, :LANES] = jnp.where(lower, taps_at, 0.0).astype(BF16)
            mr[b, here, LANES:] = jnp.where(lower, 0.0, taps_at).astype(BF16)
            tf[b, here, :] = jnp.where(lower, skew(behind[g : g + 1]), 0.0).astype(BF16)
            tb[b, here, :] = jnp.where(upper, skew(ahead[g : g + 1]), 0.0).astype(BF16)
        return carried

    lax.fori_loop(0, BLOCKS, build, 0)

    for j in range(N_DP):
        feature_own(j).wait()
        for s in range(1, N_CTX):
            feature_wait(j, s)

    def strips(owner, first=0, count=N_CTX):
        return og.at[pl.ds(first, count), strip(owner), :]

    def y_copy(owner, way, stage, first=0, count=N_CTX):
        return remote(
            strips(owner, first, count), strips(owner, first, count),
            y_send.at[way, stage], y_recv.at[way, stage], tp=tp(steps[way], core),
        )

    def sib_copy(owner, at):
        return remote(strips(owner), strips(owner), sib_send.at[at], sib_recv.at[at], tp=sibling)

    for way in range(2):
        y_copy(t, way, 0).start()
    sib_copy(t, 0).start()

    def w_relay(way):
        source = dp(-steps[way])
        rows = pl.ds(way * HALF, HALF)
        return remote(
            wg.at[source, rows, :], wg.at[source, rows, :],
            w_send.at[way, 1], w_recv.at[way, 1], dp=dp(steps[way]),
        )

    def w_relay_in(way):
        rows = pl.ds(way * HALF, HALF)
        opposite = wg.at[dp(2), rows, :]
        return remote(opposite, opposite, w_send.at[way, 1], w_recv.at[way, 1], dp=dp(steps[way]))

    halo_copy.wait_recv()

    def convolve(b, carried):
        lanes = pl.ds(pl.multiple_of(b * LANES, LANES), LANES)
        before = jnp.where(c > 0, halo[:, lanes], jnp.zeros((ROWS, LANES), BF16))
        both = jnp.concatenate([prod[:, lanes], before], axis=0)
        out = own_groups(dot(mr[b], both))
        conv[:, lanes] = out
        mix = (q_ref[:, lanes].astype(F32) * out).astype(BF16)
        mixed[:, lanes] = mix
        ends[:, lanes] = fold_modes(dot(coef_e[b], mix, a_dim=0)).astype(BF16)
        return carried

    lax.fori_loop(0, BLOCKS, convolve, 0)

    def state_copy(s):
        return remote(ends, ends_all.at[c], st_send.at[0, s], st_recv.at[0, c], ctx=ctx(s))

    for s in range(1, N_CTX):
        @pl.when(c + s < N_CTX)
        def _():
            state_copy(s).start()

    for way in range(2):
        source = dp(-steps[way])
        remote(
            w_ref, wg.at[source], w_send.at[way, 0], w_recv.at[way, 0], dp=dp(steps[way])
        ).wait_recv()
        w_relay(way).start()
    for way in range(2):
        owner = tp(-steps[way], core)
        y_copy(owner, way, 0).wait_recv()
        y_copy(owner, way, 1, way * 4, 4).start()
        sib_copy(owner, 1 + way).start()

    def local_long(b, carried):
        lanes = pl.ds(pl.multiple_of(b * LANES, LANES), LANES)
        long_out[:, lanes] = own_groups(dot(tf[b], mixed[:, lanes]))
        return carried

    lax.fori_loop(0, BLOCKS, local_long, 0)

    far = tp(2, core)
    for way in range(2):
        y_copy(far, way, 1, way * 4, 4).wait_recv()
    sib_copy(far, 3).start()

    state[...] = jnp.zeros_like(state)
    for earlier in range(N_CTX - 1):
        @pl.when(earlier < c)
        def _():
            remote(
                ends, ends_all.at[earlier], st_send.at[0, 0], st_recv.at[0, earlier], ctx=earlier
            ).wait_recv()
            for b in range(BLOCKS):
                lanes = pl.ds(b * LANES, LANES)
                state[:, lanes] = state[:, lanes] * decay[b] + ends_all[earlier, :, lanes].astype(F32)

    def finish_long(b, carried):
        lanes = pl.ds(pl.multiple_of(b * LANES, LANES), LANES)
        total = long_out[:, lanes] + modal(carry[b], state[:, lanes])
        long_out[:, lanes] = total
        gall[c, :, lanes] = (g_ref[:, lanes].astype(F32) * total).astype(BF16)
        return carried

    lax.fori_loop(0, BLOCKS, finish_long, 0)

    def ag_block(owner, half, rows):
        return gall.at[owner, rows, pl.ds(half * HALF, HALF)]

    def ag_rows(way, step):
        return pl.ds(0, ROWS) if step < 3 else pl.ds(way * 64, 64)

    def ag_copy(half, way, step):
        block = ag_block(ctx(-steps[way] * step), half, ag_rows(way, step))
        return remote(
            block, block, ag_send.at[half, way, step], ag_recv.at[half, way, step], ctx=ctx(steps[way])
        )

    def ag_in(half, way, step):
        block = ag_block(ctx(-steps[way] * (step + 1)), half, ag_rows(way, step))
        return remote(
            block, block, ag_send.at[half, way, step], ag_recv.at[half, way, step], ctx=ctx(steps[way])
        )

    for half in range(2):
        for way in range(2):
            ag_copy(half, way, 0).start()

    w_own.wait()
    for way in range(2):
        w_relay_in(way).wait_recv()
    for at, owner in enumerate(
        (sibling, tp(-1, 1 - core), tp(1, 1 - core), tp(2, 1 - core))
    ):
        sib_copy(owner, at).wait_recv()

    def project(n, carried):
        channels = pl.ds(pl.multiple_of(n * FEATS, FEATS), FEATS)
        total = jnp.zeros((N_CTX * ROWS, FEATS), F32)
        rows = og[...].reshape(N_CTX * ROWS, WIDTH)
        for j in range(N_DP):
            total = total + dot(rows[:, j * FEATS : (j + 1) * FEATS], wg[j, channels, :], b_dim=1)
        part[:, :, channels] = total.reshape(N_CTX, ROWS, FEATS)
        return carried

    lax.fori_loop(0, WIDTH // FEATS, project, 0)

    def rs_rows(way, step):
        return pl.ds(way * 64, 64) if step == 0 else pl.ds(0, ROWS)

    def rs_copy(way, step):
        rows = rs_rows(way, step)
        return remote(
            rs_out.at[way, step, rows, :], rs_in.at[way, step, rows, :],
            rs_send.at[way, step], rs_recv.at[way, step], ctx=ctx(steps[way]),
        )

    for step in range(4):
        for way in range(2):
            target = ctx(steps[way] * (4 - step))
            if step == 0:
                rows = rs_rows(way, 0)
                rs_out[way, 0, rows, :] = part[target, rows, :].astype(BF16)
            else:
                rs_copy(way, step - 1).wait_recv()
                if step == 1:
                    rows, rest = rs_rows(way, 0), rs_rows(1 - way, 0)
                    rs_out[way, 1, rows, :] = (
                        part[target, rows, :] + rs_in[way, 0, rows, :].astype(F32)
                    ).astype(BF16)
                    rs_out[way, 1, rest, :] = part[target, rest, :].astype(BF16)
                else:
                    rs_out[way, step] = (
                        part[target] + rs_in[way, step - 1].astype(F32)
                    ).astype(BF16)
            rs_copy(way, step).start()
        if step > 0:
            for half in range(2):
                for way in range(2):
                    ag_in(half, way, step - 1).wait_recv()
                    ag_copy(half, way, step).start()
        if step == 0:
            for at in range(N_CTX):
                ogt[:, at * ROWS : (at + 1) * ROWS] = og[at].T

    for way in range(2):
        rs_copy(way, 3).wait_recv()

    def seed_of(lanes):
        return delta[:, lanes] * g_ref[:, lanes].astype(F32)

    def begin_back(b, carried):
        lanes = pl.ds(pl.multiple_of(b * LANES, LANES), LANES)
        total = (
            part[c, :, lanes] + rs_in[0, 3, :, lanes].astype(F32) + rs_in[1, 3, :, lanes].astype(F32)
        )
        delta[:, lanes] = total
        gg_ref[:, lanes] = (total * long_out[:, lanes]).astype(BF16)
        seed = (total * g_ref[:, lanes].astype(F32)).astype(BF16)
        starts[:, lanes] = fold_modes(dot(coef_a[b], seed, a_dim=0)).astype(BF16)
        return carried

    lax.fori_loop(0, BLOCKS, begin_back, 0)

    def back_copy(s):
        return remote(starts, starts_all.at[c], st_send.at[1, s], st_recv.at[1, c], ctx=ctx(-s))

    for s in range(1, N_CTX):
        @pl.when(c - s >= 0)
        def _():
            back_copy(s).start()

    def weight_part(half, owner, first=0, count=FEATS):
        channels = pl.ds(half * HALF, HALF)
        rows = pl.ds(pl.multiple_of(owner * FEATS + first, 128), count)
        gated = gall[:, :, channels].reshape(N_CTX * ROWS, HALF)
        return dot(ogt[rows, :], gated)

    def x1_copy(half, way):
        return remote(
            x1_out.at[half, way], x1_in.at[half, way],
            x_send.at[half, way, 0], x_recv.at[half, way, 0], dp=dp(steps[way]),
        )

    def x2_copy(half, way):
        return remote(
            x2_out.at[half, way], x2_in.at[half, way],
            x_send.at[half, way, 1], x_recv.at[half, way, 1], dp=dp(steps[way]),
        )

    for half in range(2):
        for way in range(2):
            ag_in(half, way, 3).wait_recv()
        opposite = weight_part(half, dp(2))
        for way in range(2):
            x1_out[half, way] = opposite[way * 128 : (way + 1) * 128].astype(BF16)
            x1_copy(half, way).start()

    def local_back(b, carried):
        lanes = pl.ds(pl.multiple_of(b * LANES, LANES), LANES)
        conv_seed = seed_of(lanes).astype(BF16)
        delta[:, lanes] = own_groups(dot(tb[b], conv_seed))
        return carried

    for half in range(2):
        for way in range(2):
            near = weight_part(half, dp(steps[way]))
            x1_copy(half, way).wait_recv()
            mine, other = slice(way * 128, way * 128 + 128), slice((1 - way) * 128, (1 - way) * 128 + 128)
            x2_out[half, way, mine, :] = (near[mine] + x1_in[half, way].astype(F32)).astype(BF16)
            x2_out[half, way, other, :] = near[other].astype(BF16)
            x2_copy(half, way).start()
        if half == 0:
            lax.fori_loop(0, BLOCKS, local_back, 0)

    state[...] = jnp.zeros_like(state)
    for later in range(N_CTX - 1, 0, -1):
        @pl.when(later > c)
        def _():
            remote(
                starts, starts_all.at[later], st_send.at[1, 0], st_recv.at[1, later], ctx=later
            ).wait_recv()
            for b in range(BLOCKS):
                lanes = pl.ds(b * LANES, LANES)
                state[:, lanes] = state[:, lanes] * decay[b] + starts_all[later, :, lanes].astype(F32)

    def finish_back(b, carried):
        lanes = pl.ds(pl.multiple_of(b * LANES, LANES), LANES)
        total = delta[:, lanes] + modal(back[b], state[:, lanes])
        qg_ref[:, lanes] = (total * conv[:, lanes]).astype(BF16)
        cg_ref[:, lanes] = (total * q_ref[:, lanes].astype(F32)).astype(BF16)
        return carried

    lax.fori_loop(0, BLOCKS, finish_back, 0)

    for half in range(2):
        own = weight_part(half, d)
        for way in range(2):
            x2_copy(half, way).wait_recv()
            own = own + x2_in[half, way].astype(F32)
        wt_ref[:, half * HALF : (half + 1) * HALF] = own.astype(BF16)

    for s in range(1, N_CTX):
        for j in range(N_DP):
            feature_copy(j, s).wait_send()

        @pl.when(c + s < N_CTX)
        def _():
            state_copy(s).wait_send()

        @pl.when(c - s >= 0)
        def _():
            back_copy(s).wait_send()
    halo_copy.wait_send()
    for way in range(2):
        remote(w_ref, wg.at[d], w_send.at[way, 0], w_recv.at[way, 0], dp=dp(steps[way])).wait_send()
        w_relay(way).wait_send()
        y_copy(t, way, 0).wait_send()
        y_copy(tp(-steps[way], core), way, 1, way * 4, 4).wait_send()
        for step in range(4):
            rs_copy(way, step).wait_send()
            for half in range(2):
                ag_copy(half, way, step).wait_send()
        for half in range(2):
            x1_copy(half, way).wait_send()
            x2_copy(half, way).wait_send()
    for at, owner in enumerate((t, tp(-1, core), tp(1, core), far)):
        sib_copy(owner, at).wait_send()


def on_device(*args):
    vmem = pl.BlockSpec(memory_space=pltpu.VMEM)
    hbm = pl.BlockSpec(memory_space=pl.ANY)
    act = jax.ShapeDtypeStruct((ROWS, WIDTH), BF16)
    dma = pltpu.SemaphoreType.DMA
    stacked = (BLOCKS, 8 * ROWS, LANES)
    return pl.pallas_call(
        kernel,
        out_shape=(act, act, act, jax.ShapeDtypeStruct((FEATS, WIDTH), BF16)),
        in_specs=[vmem, vmem, vmem, vmem, hbm, hbm, vmem, vmem, vmem],
        out_specs=(vmem, vmem, vmem, vmem),
        scratch_shapes=[
            pltpu.VMEM((ROWS, WIDTH), BF16),
            pltpu.VMEM((ROWS, WIDTH), BF16),
            pltpu.VMEM((N_CTX, ROWS, WIDTH), BF16),
            pltpu.VMEM((N_DP, WIDTH, FEATS), BF16),
            pltpu.VMEM((BLOCKS, 8 * ROWS, 2 * LANES), BF16),
            pltpu.VMEM(stacked, BF16),
            pltpu.VMEM(stacked, BF16),
            pltpu.VMEM((WIDTH // GROUP, LANES), F32),
            pltpu.VMEM((BLOCKS, ROWS, LANES), BF16),
            pltpu.VMEM((BLOCKS, ROWS, LANES), BF16),
            pltpu.VMEM((BLOCKS, ROWS, LANES), F32),
            pltpu.VMEM((BLOCKS, ROWS, LANES), F32),
            pltpu.VMEM((BLOCKS, ORDER, LANES), F32),
            pltpu.VMEM((ROWS, WIDTH), F32),
            pltpu.VMEM((ROWS, WIDTH), BF16),
            pltpu.VMEM((ROWS, WIDTH), F32),
            pltpu.VMEM((N_CTX, ROWS, WIDTH), F32),
            pltpu.VMEM((ORDER, WIDTH), BF16),
            pltpu.VMEM((N_CTX, ORDER, WIDTH), BF16),
            pltpu.VMEM((ORDER, WIDTH), BF16),
            pltpu.VMEM((N_CTX, ORDER, WIDTH), BF16),
            pltpu.VMEM((ORDER, WIDTH), F32),
            pltpu.VMEM((2, 4, ROWS, WIDTH), BF16),
            pltpu.VMEM((2, 4, ROWS, WIDTH), BF16),
            pltpu.VMEM((N_CTX, ROWS, WIDTH), BF16),
            pltpu.VMEM((ROWS, WIDTH), F32),
            pltpu.VMEM((WIDTH, N_CTX * ROWS), BF16),
            pltpu.VMEM((2, 2, 128, HALF), BF16),
            pltpu.VMEM((2, 2, 128, HALF), BF16),
            pltpu.VMEM((2, 2, FEATS, HALF), BF16),
            pltpu.VMEM((2, 2, FEATS, HALF), BF16),
            dma((N_CTX, N_DP)), dma((N_CTX, N_DP)), dma((N_DP + 1,)), dma((2,)),
            dma((2, 2)), dma((2, 2)), dma((2, 2)), dma((2, 2)), dma((4,)), dma((4,)),
            dma((2, N_CTX)), dma((2, N_CTX)), dma((2, 4)), dma((2, 4)),
            dma((2, 2, 4)), dma((2, 2, 4)), dma((2, 2, 2)), dma((2, 2, 2)),
        ],
        compiler_params=pltpu.CompilerParams(
            collective_id=0, has_side_effects=True, vmem_limit_bytes=56 * 1024 * 1024
        ),
        name="hyena_backward",
    )(*args)


def solution(mesh):
    rows = P(("dp", "ctx"), "tp")
    return jax.shard_map(
        on_device,
        mesh=mesh,
        in_specs=(
            rows, rows, rows, rows, P(("dp", "ctx"), None), P("tp", ("dp", "ctx")),
            P("tp", None), P("tp", None), P("tp", None),
        ),
        out_specs=(rows, rows, rows, rows),
        check_vma=False,
    )
```

time: 561 us -> 109 us (0.19)
  waiting for transfers between devices: 223 us -> 0 us
  local copies, waits for them, and re-layouts: 223 us -> 9.66 us
  Pallas kernels: 0 us -> 96.8 us
  starting transfers between devices: 44.8 us -> 0 us
  matrix products: 43.7 us -> 0 us
  between operations: 14.3 us -> 0.64 us
  other arithmetic: 8.61 us -> 0 us
    gather x4 -> x0, local copies, waits for them, and re-layouts: 197 us -> none  [the longest x2 135 us: mr_matrix(): picked = jnp.take(filters, jnp.clip(lag_index, 0, taps - 1), axis=1)]
    reduce_scatter x1 -> x0, waiting for transfers between devices: 167 us -> none  [on_device(): lax.psum_scatter(lax.dot_general(columns, gated, (((0,), (0,)), ((), ()))...]
    pallas_call x0 -> x1, Pallas kernels: none -> 96.8 us  [on_device(): pl.pallas_call(kernel, out_shape=(act, act, act, jax.ShapeDtypeStruct((FE...]
    ppermute x15 -> x0, waiting for transfers between devices: 55.3 us -> none  [shifted(): lax.ppermute(value, axis, [(source, source + steps) for source in range(l...]
    ppermute x15 -> x0, starting transfers between devices: 44.8 us -> none  [shifted(): lax.ppermute(value, axis, [(source, source + steps) for source in range(l...]
    dot_general x9 -> x0, matrix products: 43.7 us -> none  [the longest x1 12.4 us: on_device(): lax.dot_general(columns, lax.all_gather(proj_weight, ('dp', 'ctx'), axis=...]
    reshape x17 -> x0, local copies, waits for them, and re-layouts: 7.86 us -> none  [the longest x14 3.79 us: on_device(): decay_full = jnp.repeat(block_decay, GROUP, axis=1)]
  transfers between devices with their start and end apart: 17 -> 0, of which waited for: 15 -> 0; matrix products, arithmetic and copies ran while one was open for 49% -> 0% of each run, Pallas kernels for 0% -> 0%
where the time goes in v1:
time: 109 us; the launch traced here: 107 us
  Pallas kernels  96.8 us (89%)
  local copies, waits for them, and re-layouts  9.66 us (9%)
    pallas_call x1, Pallas kernels, on_device(): pl.pallas_call(kernel, out_shape=(act, act, act, jax.ShapeDtypeStruct((FE...  96.8 us
    unnamed x6, local copies, waits for them, and re-layouts  9.66 us

profile of v1, /device:TPU:8, one launch (start us, length us, event | category | flops | bytes accessed | tf_op | source)
XLA Modules:
  0.0 107.1 jit_solution(11865311973262527176)
XLA Ops:
  0.6 1.4 %copy.13.rate_ref = f32[64,16]{1,0:T(8,128)} copy(f32[64,16]{0,1:T(8,128)} %param.16) | data formatting | bytes 8192 | tf_op args[7]
  2.0 1.4 %copy.14.res_ref = f32[64,16]{1,0:T(8,128)} copy(f32[64,16]{0,1:T(8,128)} %param.17) | data formatting | bytes 8192 | tf_op args[8]
  3.4 96.8 %hyena_backward.1 = (bf16[128,1024]{1,0:T(8,128)(2,1)}, bf16[128,1024]{1,0:T(8,128)(2,1)}, bf16[128,1024]{1,0:T(8,128)(2,1)}, bf16[256,1024]{1,0:T(8,128)(2,1)}) custom-call(bf16[128,1024]{1,0:T(8,128)(2,1)} %q_ref.1, bf16[128,1024]{1,0:T(8,128)(2,1)} %k_ref.1, bf16[128,1024]{1,0:T(8,128)(2,1)} %v_ref.1, bf16[128,1024]{1,0:T(8,128)(2,1)} %g_ref.1, ...), custom_call_target="tpu_custom_call" | custom-call | tf_op jit(solution)/shard_map/hyena_backward/pallas_call | solution.py:500
  100.3 1.7 %copy.19 = bf16[128,1024]{1,0:T(8,128)(2,1)} copy(bf16[128,1024]{1,0:T(8,128)(2,1)} %get-tuple-element.8) | data formatting | bytes 524288
  101.9 1.7 %copy.20 = bf16[128,1024]{1,0:T(8,128)(2,1)} copy(bf16[128,1024]{1,0:T(8,128)(2,1)} %get-tuple-element.9) | data formatting | bytes 524288
  103.6 1.7 %copy.21 = bf16[128,1024]{1,0:T(8,128)(2,1)} copy(bf16[128,1024]{1,0:T(8,128)(2,1)} %get-tuple-element.10) | data formatting | bytes 524288
  105.3 1.9 %copy.22 = bf16[256,1024]{1,0:T(8,128)(2,1)} copy(bf16[256,1024]{1,0:T(8,128)(2,1)} %get-tuple-element.11) | data formatting | bytes 1048576

commit v2 on v1

v2 whole, which is shorter than its diff:
```python
import jax
import jax.numpy as jnp
from jax import lax
from jax.experimental import pallas as pl
from jax.experimental.pallas import tpu as pltpu
from jax.sharding import PartitionSpec as P

GROUP = 16
ORDER = 16
ROWS = 128
WIDTH = 1024
LANES = 128
BLOCKS = WIDTH // LANES
N_DP = 4
N_CTX = 8
N_Y = 4
FEATS = 256
HALF = WIDTH // 2
HALF_BLOCKS = BLOCKS // 2

MESH = pl.DeviceIdType.MESH
HIGHEST = lax.Precision.HIGHEST
BF16 = jnp.bfloat16
F32 = jnp.float32


def remote(src, dst, send, recv, **device):
    return pltpu.make_async_remote_copy(
        src_ref=src, dst_ref=dst, send_sem=send, recv_sem=recv, device_id=device, device_id_type=MESH
    )


def iota(dim, shape=(ROWS, LANES)):
    return lax.broadcasted_iota(jnp.int32, shape, dim)


def skew(row):
    return pltpu.roll(jnp.broadcast_to(row, (ROWS, LANES)), 0, 1, stride=1, stride_axis=0)


def dot(a, b, a_dim=1, b_dim=0, precision=None):
    return lax.dot_general(
        a, b, (((a_dim,), (b_dim,)), ((), ())), precision=precision, preferred_element_type=F32
    )


def own_groups(stacked):
    lane_group = iota(1) // GROUP
    total = jnp.zeros((ROWS, LANES), F32)
    for g in range(LANES // GROUP):
        total = jnp.where(lane_group == g, stacked[g * ROWS : (g + 1) * ROWS], total)
    return total


def fold_modes(modes):
    own = jnp.where(iota(0) // ORDER == iota(1) // GROUP, modes, 0.0)
    total = own[:ORDER]
    for g in range(1, LANES // GROUP):
        total = total + own[g * ORDER : (g + 1) * ORDER]
    return total


def split(value):
    high = value.astype(BF16)
    return high, (value - high.astype(F32)).astype(BF16)


def modal(coef, state):
    spread = jnp.where(
        iota(0) // ORDER == iota(1) // GROUP, jnp.concatenate([state] * (LANES // GROUP), axis=0), 0.0
    )
    coef_high, coef_low = split(coef)
    state_high, state_low = split(spread)
    return dot(coef_high, state_high) + dot(coef_high, state_low) + dot(coef_low, state_high)


def kernel(
    q_ref, k_ref, v_ref, g_ref, og_ref, w_ref, f_ref, rate_ref, res_ref,
    qg_ref, cg_ref, gg_ref, wt_ref,
    prod, halo, og, wg, mr, tf, tb, base, rates_all, weights_all, coef_a, coef_e, carry, back, decay,
    conv, mixed, long_out, part, ends, ends_all, starts, starts_all, state,
    rs_out, rs_in, gall, delta, ogt, x_out, x_in,
    a2_send, a2_recv, loc, halo_send, halo_recv, w_send, w_recv, y_send, y_recv, sib_send, sib_recv,
    st_send, st_recv, rs_send, rs_recv, ag_send, ag_recv, x_send, x_recv,
):
    d, c, t = lax.axis_index("dp"), lax.axis_index("ctx"), lax.axis_index("tp")
    y, core = t // 2, t % 2
    halves = [pl.ds(half * HALF, HALF) for half in range(2)]
    steps = (1, -1)

    def ctx(step):
        return lax.rem(c + step + N_CTX, N_CTX)

    def dp(step):
        return lax.rem(d + step + N_DP, N_DP)

    def tp(step, side):
        return lax.rem(y + step + N_Y, N_Y) * 2 + side

    sibling = tp(0, 1 - core)

    barrier = pltpu.get_barrier_semaphore()
    for s in range(1, N_CTX):
        pl.semaphore_signal(barrier, inc=1, device_id={"ctx": ctx(s)}, device_id_type=MESH)
    for s in range(1, N_DP):
        pl.semaphore_signal(barrier, inc=1, device_id={"dp": dp(s)}, device_id_type=MESH)
    for s in range(1, N_Y):
        pl.semaphore_signal(barrier, inc=1, device_id={"tp": tp(s, core)}, device_id_type=MESH)
    pl.semaphore_signal(barrier, inc=1, device_id={"tp": sibling}, device_id_type=MESH)
    prod[...] = (k_ref[...].astype(F32) * v_ref[...].astype(F32)).astype(BF16)
    pl.semaphore_wait(barrier, (N_CTX - 1) + (N_DP - 1) + (N_Y - 1) + 1)

    def strip(owner):
        return pl.ds(pl.multiple_of(owner * 16, 16), 16)

    def feature_copy(j, s):
        to = ctx(s)
        return remote(
            og_ref.at[strip(t), pl.ds(pl.multiple_of((j * N_CTX + to) * FEATS, FEATS), FEATS)],
            og.at[c, strip(t), pl.ds(j * FEATS, FEATS)],
            a2_send.at[s, j], a2_recv.at[c, j], ctx=to,
        )

    def feature_wait(j, s):
        source = ctx(s)
        remote(
            og_ref.at[strip(t), pl.ds(j * FEATS, FEATS)], og.at[source, strip(t), pl.ds(j * FEATS, FEATS)],
            a2_send.at[s, j], a2_recv.at[source, j], ctx=source,
        ).wait_recv()

    def feature_own(j):
        return pltpu.make_async_copy(
            og_ref.at[strip(t), pl.ds(pl.multiple_of((j * N_CTX + c) * FEATS, FEATS), FEATS)],
            og.at[c, strip(t), pl.ds(j * FEATS, FEATS)], loc.at[j],
        )

    def halo_copy(half):
        lanes = halves[half]
        return remote(prod.at[:, lanes], halo.at[:, lanes], halo_send.at[half], halo_recv.at[half], ctx=ctx(1))

    def w_copy(half, s):
        rows = halves[half]
        return remote(
            w_ref.at[rows, :], wg.at[d, rows, :], w_send.at[half, s], w_recv.at[half, s], dp=dp(s)
        )

    def w_in(half, s):
        rows = halves[half]
        return remote(
            w_ref.at[rows, :], wg.at[dp(-s), rows, :], w_send.at[half, s], w_recv.at[half, s], dp=dp(s)
        )

    halo_copy(0).start()
    for s in (4, 3, 5, 2, 6, 1, 7):
        for j in range(N_DP):
            feature_copy(j, s).start()
    halo_copy(1).start()
    for j in range(N_DP):
        feature_own(j).start()
    for half in range(2):
        for s in (2, 1, 3):
            w_copy(half, s).start()
    w_own = pltpu.make_async_copy(w_ref, wg.at[d], loc.at[N_DP])
    w_own.start()

    repeat_modes = (iota(1, (ORDER, LANES)) % ORDER == iota(0, (ORDER, LANES))).astype(F32)
    base[...] = dot(f_ref[...], ((iota(0) + iota(1)) % LANES == 0).astype(BF16))
    rates_all[...] = dot(rate_ref[...], repeat_modes, a_dim=0, precision=HIGHEST)
    weights_all[...] = dot(res_ref[...], repeat_modes, a_dim=0, precision=HIGHEST)

    def eight(b):
        return pl.ds(pl.multiple_of(b * 8, 8), 8)

    def lanes_of(b):
        return pl.ds(pl.multiple_of(b * LANES, LANES), LANES)

    def own_lane():
        return iota(1, (8, LANES)) // GROUP == iota(0, (8, LANES))

    def modes(b):
        rate = jnp.sum(jnp.where(own_lane(), rates_all[eight(b), :], 0.0), axis=0, keepdims=True)
        weights = jnp.where(own_lane(), weights_all[eight(b), :], 0.0)
        return rate, weights, jnp.sum(weights, axis=0, keepdims=True)

    def build_mr(b, carried):
        taps = base[eight(b), :]
        lower = iota(0) >= iota(1)
        for g in range(8):
            here = pl.ds(g * ROWS, ROWS)
            taps_at = skew(taps[g : g + 1])
            mr[b, here, :LANES] = jnp.where(lower, taps_at, 0.0).astype(BF16)
            mr[b, here, LANES:] = jnp.where(lower, 0.0, taps_at).astype(BF16)
        rate, _, _ = modes(b)
        coef_e[b] = jnp.exp(-rate * (ROWS - 1.0 - iota(0).astype(F32))).astype(BF16)
        return carried

    def build_forward(b, carried):
        rate, weights, weight = modes(b)
        row_at = iota(0).astype(F32)
        lag = jnp.where(iota(0) == 0, 0.0, ROWS - row_at)
        carry[b] = weight * jnp.exp(-rate * (row_at + 1.0))
        per_mode = jnp.where(iota(1, (ORDER, LANES)) % ORDER == iota(0, (ORDER, LANES)), rate, 0.0)
        to_channels = (iota(0) // ORDER == iota(1) // GROUP).astype(F32)
        decay[b] = jnp.exp(-ROWS * dot(per_mode, to_channels, precision=HIGHEST))
        behind = dot(weights, jnp.exp(-rate * lag), b_dim=1, precision=HIGHEST)
        lower = iota(0) >= iota(1)
        for g in range(8):
            tf[b, pl.ds(g * ROWS, ROWS), :] = jnp.where(lower, skew(behind[g : g + 1]), 0.0).astype(BF16)
        return carried

    def build_back(b, carried):
        rate, weights, weight = modes(b)
        row_at = iota(0).astype(F32)
        falling = jnp.exp(-rate * row_at)
        coef_a[b] = falling.astype(BF16)
        back[b] = weight * jnp.exp(-rate * (ROWS - row_at))
        ahead = dot(weights, falling, b_dim=1, precision=HIGHEST)
        upper = iota(1) >= iota(0)
        for g in range(8):
            tb[b, pl.ds(g * ROWS, ROWS), :] = jnp.where(upper, skew(ahead[g : g + 1]), 0.0).astype(BF16)
        return carried

    def each(half, function):
        lax.fori_loop(half * HALF_BLOCKS, (half + 1) * HALF_BLOCKS, function, 0)

    def convolve(b, carried):
        lanes = lanes_of(b)
        before = jnp.where(c > 0, halo[:, lanes], jnp.zeros((ROWS, LANES), BF16))
        both = jnp.concatenate([prod[:, lanes], before], axis=0)
        out = own_groups(dot(mr[b], both))
        conv[:, lanes] = out
        mix = (q_ref[:, lanes].astype(F32) * out).astype(BF16)
        mixed[:, lanes] = mix
        ends[:, lanes] = fold_modes(dot(coef_e[b], mix, a_dim=0)).astype(BF16)
        return carried

    def state_copy(half, s):
        lanes = halves[half]
        return remote(
            ends.at[:, lanes], ends_all.at[c, :, lanes], st_send.at[0, half, s], st_recv.at[0, half, c], ctx=ctx(s)
        )

    def state_in(half, source):
        lanes = halves[half]
        return remote(
            ends.at[:, lanes], ends_all.at[source, :, lanes], st_send.at[0, half, 0], st_recv.at[0, half, source],
            ctx=source,
        )

    def back_copy(half, s):
        lanes = halves[half]
        return remote(
            starts.at[:, lanes], starts_all.at[c, :, lanes], st_send.at[1, half, s], st_recv.at[1, half, c],
            ctx=ctx(-s),
        )

    def back_in(half, source):
        lanes = halves[half]
        return remote(
            starts.at[:, lanes], starts_all.at[source, :, lanes], st_send.at[1, half, 0],
            st_recv.at[1, half, source], ctx=source,
        )

    def gather_states(half, incoming, received, order, wanted):
        state[:, halves[half]] = jnp.zeros((ORDER, HALF), F32)
        for source in order:
            @pl.when(wanted(source))
            def _():
                incoming(half, source).wait_recv()
                for b in range(half * HALF_BLOCKS, (half + 1) * HALF_BLOCKS):
                    lanes = pl.ds(b * LANES, LANES)
                    state[:, lanes] = state[:, lanes] * decay[b] + received[source, :, lanes].astype(F32)

    def local_long(b, carried):
        lanes = lanes_of(b)
        long_out[:, lanes] = own_groups(dot(tf[b], mixed[:, lanes]))
        return carried

    def finish_long(b, carried):
        lanes = lanes_of(b)
        total = long_out[:, lanes] + modal(carry[b], state[:, lanes])
        long_out[:, lanes] = total
        gall[c, :, lanes] = (g_ref[:, lanes].astype(F32) * total).astype(BF16)
        return carried

    def ag_block(half, way, step, ahead):
        rows = pl.ds(0, ROWS) if step < 3 else pl.ds(way * 64, 64)
        return gall.at[ctx(-steps[way] * (step + ahead)), rows, halves[half]]

    def ag_copy(half, way, step, ahead=0):
        block = ag_block(half, way, step, ahead)
        return remote(
            block, block, ag_send.at[half, way, step], ag_recv.at[half, way, step], ctx=ctx(steps[way])
        )

    def gather(half, step):
        for way in range(2):
            if step > 0:
                ag_copy(half, way, step - 1, 1).wait_recv()
            if step < 4:
                ag_copy(half, way, step).start()

    def rs_rows(way, step):
        return pl.ds(way * 64, 64) if step == 0 else pl.ds(0, ROWS)

    def rs_copy(half, way, step):
        rows = rs_rows(way, step)
        return remote(
            rs_out.at[half, way, step, rows, :], rs_in.at[half, way, step, rows, :],
            rs_send.at[half, way, step], rs_recv.at[half, way, step], ctx=ctx(steps[way]),
        )

    def reduce(half, step):
        lanes = halves[half]
        for way in range(2):
            if step > 0:
                rs_copy(half, way, step - 1).wait_recv()
            if step == 4:
                continue
            target = ctx(steps[way] * (4 - step))
            if step < 2:
                rows, rest = rs_rows(way, 0), rs_rows(1 - way, 0)
                total = part[target, rows, lanes]
                if step == 1:
                    total = total + rs_in[half, way, 0, rows, :].astype(F32)
                    rs_out[half, way, 1, rest, :] = part[target, rest, lanes].astype(BF16)
                rs_out[half, way, step, rows, :] = total.astype(BF16)
            else:
                rs_out[half, way, step] = (
                    part[target, :, lanes] + rs_in[half, way, step - 1].astype(F32)
                ).astype(BF16)
            rs_copy(half, way, step).start()

    def project(n, carried):
        channels = pl.ds(pl.multiple_of(n * FEATS, FEATS), FEATS)
        total = jnp.zeros((N_CTX * ROWS, FEATS), F32)
        rows = og[...].reshape(N_CTX * ROWS, WIDTH)
        for j in range(N_DP):
            total = total + dot(rows[:, j * FEATS : (j + 1) * FEATS], wg[j, channels, :], b_dim=1)
        part[:, :, channels] = total.reshape(N_CTX, ROWS, FEATS)
        return carried

    def project_half(half):
        for s in range(1, N_DP):
            w_in(half, s).wait_recv()
        lax.fori_loop(half * 2, half * 2 + 2, project, 0)

    def begin_back_of(half):
        def begin_back(b, carried):
            lanes = lanes_of(b)
            inner = pl.ds(pl.multiple_of((b - half * HALF_BLOCKS) * LANES, LANES), LANES)
            total = (
                part[c, :, lanes]
                + rs_in[half, 0, 3, :, inner].astype(F32)
                + rs_in[half, 1, 3, :, inner].astype(F32)
            )
            delta[:, lanes] = total
            gg_ref[:, lanes] = (total * long_out[:, lanes]).astype(BF16)
            seed = (total * g_ref[:, lanes].astype(F32)).astype(BF16)
            starts[:, lanes] = fold_modes(dot(coef_a[b], seed, a_dim=0)).astype(BF16)
            return carried

        each(half, begin_back)
        for s in range(1, N_CTX):
            @pl.when(c - s >= 0)
            def _():
                back_copy(half, s).start()

    def local_back(b, carried):
        lanes = lanes_of(b)
        seed = (delta[:, lanes] * g_ref[:, lanes].astype(F32)).astype(BF16)
        delta[:, lanes] = own_groups(dot(tb[b], seed))
        return carried

    def finish_back(b, carried):
        lanes = lanes_of(b)
        total = delta[:, lanes] + modal(back[b], state[:, lanes])
        qg_ref[:, lanes] = (total * conv[:, lanes]).astype(BF16)
        cg_ref[:, lanes] = (total * q_ref[:, lanes].astype(F32)).astype(BF16)
        return carried

    def weight_part(half, owner):
        rows = pl.ds(pl.multiple_of(owner * FEATS, FEATS), FEATS)
        return dot(ogt[rows, :], gall[:, :, halves[half]].reshape(N_CTX * ROWS, HALF))

    def x_copy(half, s):
        return remote(
            x_out.at[half, s - 1], x_in.at[half, s - 1], x_send.at[half, s], x_recv.at[half, s], dp=dp(s)
        )

    def weight_send(half):
        for s in (2, 1, 3):
            x_out[half, s - 1] = weight_part(half, dp(s)).astype(BF16)
            x_copy(half, s).start()

    def weight_finish(half):
        own = weight_part(half, d)
        for s in range(1, N_DP):
            x_copy(half, s).wait_recv()
            own = own + x_in[half, s - 1].astype(F32)
        wt_ref[:, half * HALF : (half + 1) * HALF] = own.astype(BF16)

    def strips(owner):
        return og.at[:, strip(owner), :]

    def y_copy(owner, s):
        return remote(strips(owner), strips(owner), y_send.at[s], y_recv.at[s], tp=tp(s, core))

    def sib_copy(owner, at):
        return remote(strips(owner), strips(owner), sib_send.at[at], sib_recv.at[at], tp=sibling)

    def begin_forward(half):
        halo_copy(half).wait_recv()
        each(half, convolve)
        for s in range(1, N_CTX):
            @pl.when(c + s < N_CTX)
            def _():
                state_copy(half, s).start()

    def forward(half):
        each(half, local_long)
        gather_states(half, state_in, ends_all, range(N_CTX - 1), lambda source: source < c)
        each(half, finish_long)
        gather(half, 0)

    def begin_y():
        for j in range(N_DP):
            feature_own(j).wait()
            for s in range(1, N_CTX):
                feature_wait(j, s)
        for s in (2, 1, 3):
            y_copy(t, s).start()
        sib_copy(t, 0).start()

    def forward_y():
        for s in range(1, N_Y):
            owner = tp(-s, core)
            y_copy(owner, s).wait_recv()
            sib_copy(owner, s).start()

    def transpose_rows(at, carried):
        ogt[:, pl.ds(pl.multiple_of(at * ROWS, ROWS), ROWS)] = og[at].T
        return carried

    each(0, build_mr)
    begin_forward(0)
    each(1, build_mr)
    each(0, build_forward)
    begin_y()
    begin_forward(1)
    forward(0)
    each(1, build_forward)
    forward(1)
    gather(0, 1)
    gather(1, 1)
    forward_y()
    each(0, build_back)
    gather(0, 2)
    each(1, build_back)
    gather(1, 2)
    w_own.wait()
    for s in range(N_Y):
        sib_copy(tp(-s, 1 - core), s).wait_recv()
    project_half(0)
    reduce(0, 0)
    gather(0, 3)
    project_half(1)
    reduce(1, 0)
    gather(1, 3)
    reduce(0, 1)
    lax.fori_loop(0, N_CTX, transpose_rows, 0)
    reduce(1, 1)
    gather(0, 4)
    weight_send(0)
    reduce(0, 2)
    gather(1, 4)
    reduce(1, 2)
    weight_send(1)
    reduce(0, 3)
    reduce(1, 3)
    reduce(0, 4)
    begin_back_of(0)
    each(0, local_back)
    weight_finish(0)
    reduce(1, 4)
    begin_back_of(1)
    each(1, local_back)
    gather_states(0, back_in, starts_all, range(N_CTX - 1, 0, -1), lambda source: source > c)
    each(0, finish_back)
    weight_finish(1)
    gather_states(1, back_in, starts_all, range(N_CTX - 1, 0, -1), lambda source: source > c)
    each(1, finish_back)

    for s in range(1, N_CTX):
        for j in range(N_DP):
            feature_copy(j, s).wait_send()

        @pl.when(c + s < N_CTX)
        def _():
            for half in range(2):
                state_copy(half, s).wait_send()

        @pl.when(c - s >= 0)
        def _():
            for half in range(2):
                back_copy(half, s).wait_send()
    for s in range(1, N_Y):
        y_copy(t, s).wait_send()
    for s in range(N_Y):
        sib_copy(tp(-s, core), s).wait_send()
    for half in range(2):
        halo_copy(half).wait_send()
        for s in range(1, N_DP):
            w_copy(half, s).wait_send()
            x_copy(half, s).wait_send()
        for way in range(2):
            for step in range(4):
                rs_copy(half, way, step).wait_send()
                ag_copy(half, way, step).wait_send()


def copy_out(*refs):
    count = len(refs) // 3
    results, outs, held, sems = refs[:count], refs[count : 2 * count], refs[2 * count : -1], refs[-1]
    arrive = [pltpu.make_async_copy(results[i], held[i], sems.at[0, i]) for i in range(count)]
    leave = [pltpu.make_async_copy(held[i], outs[i], sems.at[1, i]) for i in range(count)]
    for copy in arrive:
        copy.start()
    for i in range(count):
        arrive[i].wait()
        leave[i].start()
    for copy in leave:
        copy.wait()


def on_device(query, key_in, value_in, gate, out_grad, proj_weight, mr_filter, lr_rate, lr_residue):
    vmem = pl.BlockSpec(memory_space=pltpu.VMEM)
    hbm = pl.BlockSpec(memory_space=pl.ANY)
    act = jax.ShapeDtypeStruct((ROWS, WIDTH), BF16)
    outs = (act, act, act, jax.ShapeDtypeStruct((FEATS, WIDTH), BF16))
    dma = pltpu.SemaphoreType.DMA
    stacked = (BLOCKS, 8 * ROWS, LANES)
    results = pl.pallas_call(
        kernel,
        out_shape=outs,
        in_specs=[vmem, vmem, vmem, vmem, hbm, hbm, vmem, vmem, vmem],
        out_specs=(vmem, vmem, vmem, vmem),
        scratch_shapes=[
            pltpu.VMEM((ROWS, WIDTH), BF16),
            pltpu.VMEM((ROWS, WIDTH), BF16),
            pltpu.VMEM((N_CTX, ROWS, WIDTH), BF16),
            pltpu.VMEM((N_DP, WIDTH, FEATS), BF16),
            pltpu.VMEM((BLOCKS, 8 * ROWS, 2 * LANES), BF16),
            pltpu.VMEM(stacked, BF16),
            pltpu.VMEM(stacked, BF16),
            pltpu.VMEM((WIDTH // GROUP, LANES), F32),
            pltpu.VMEM((WIDTH // GROUP, LANES), F32),
            pltpu.VMEM((WIDTH // GROUP, LANES), F32),
            pltpu.VMEM((BLOCKS, ROWS, LANES), BF16),
            pltpu.VMEM((BLOCKS, ROWS, LANES), BF16),
            pltpu.VMEM((BLOCKS, ROWS, LANES), F32),
            pltpu.VMEM((BLOCKS, ROWS, LANES), F32),
            pltpu.VMEM((BLOCKS, ORDER, LANES), F32),
            pltpu.VMEM((ROWS, WIDTH), F32),
            pltpu.VMEM((ROWS, WIDTH), BF16),
            pltpu.VMEM((ROWS, WIDTH), F32),
            pltpu.VMEM((N_CTX, ROWS, WIDTH), F32),
            pltpu.VMEM((ORDER, WIDTH), BF16),
            pltpu.VMEM((N_CTX, ORDER, WIDTH), BF16),
            pltpu.VMEM((ORDER, WIDTH), BF16),
            pltpu.VMEM((N_CTX, ORDER, WIDTH), BF16),
            pltpu.VMEM((ORDER, WIDTH), F32),
            pltpu.VMEM((2, 2, 4, ROWS, HALF), BF16),
            pltpu.VMEM((2, 2, 4, ROWS, HALF), BF16),
            pltpu.VMEM((N_CTX, ROWS, WIDTH), BF16),
            pltpu.VMEM((ROWS, WIDTH), F32),
            pltpu.VMEM((WIDTH, N_CTX * ROWS), BF16),
            pltpu.VMEM((2, N_DP - 1, FEATS, HALF), BF16),
            pltpu.VMEM((2, N_DP - 1, FEATS, HALF), BF16),
            dma((N_CTX, N_DP)), dma((N_CTX, N_DP)), dma((N_DP + 1,)), dma((2,)), dma((2,)),
            dma((2, N_DP)), dma((2, N_DP)), dma((N_Y,)), dma((N_Y,)), dma((N_Y,)), dma((N_Y,)),
            dma((2, 2, N_CTX)), dma((2, 2, N_CTX)), dma((2, 2, 4)), dma((2, 2, 4)),
            dma((2, 2, 4)), dma((2, 2, 4)), dma((2, N_DP)), dma((2, N_DP)),
        ],
        compiler_params=pltpu.CompilerParams(
            collective_id=0, has_side_effects=True, vmem_limit_bytes=56 * 1024 * 1024
        ),
        name="hyena_backward",
    )(query, key_in, value_in, gate, out_grad, proj_weight, mr_filter, lr_rate.T, lr_residue.T)
    return pl.pallas_call(
        copy_out,
        out_shape=outs,
        in_specs=[hbm] * 4,
        out_specs=(hbm,) * 4,
        scratch_shapes=[pltpu.VMEM(out.shape, out.dtype) for out in outs] + [dma((2, 4))],
        name="copy_out",
    )(*results)


def solution(mesh):
    rows = P(("dp", "ctx"), "tp")
    return jax.shard_map(
        on_device,
        mesh=mesh,
        in_specs=(
            rows, rows, rows, rows, P(("dp", "ctx"), None), P("tp", ("dp", "ctx")),
            P("tp", None), P("tp", None), P("tp", None),
        ),
        out_specs=(rows, rows, rows, rows),
        check_vma=False,
    )
```

time: 109 us -> 83.2 us (0.76); the launches traced: 107 us -> 82.5 us
  Pallas kernels: 96.8 us -> 81.9 us
  local copies, waits for them, and re-layouts: 9.66 us -> 0 us
    pallas_call x1 -> x2, Pallas kernels: 96.8 us -> 81.9 us  [the longest x1 79.7 us: on_device(): pl.pallas_call(kernel, out_shape=outs, in_specs=[vmem, vmem, vmem, vmem,...]
    unnamed x6 -> x0, local copies, waits for them, and re-layouts: 9.66 us -> none
where the time goes in v2:
time: 83.2 us; the launch traced here: 82.5 us
  Pallas kernels  81.9 us (98%)
    pallas_call x1, Pallas kernels, on_device(): pl.pallas_call(kernel, out_shape=outs, in_specs=[vmem, vmem, vmem, vmem,...  79.7 us
    pallas_call x1, Pallas kernels, on_device(): pl.pallas_call(copy_out, out_shape=outs, in_specs=[hbm] * 4, out_specs=(h...  2.15 us

profile of v2, /device:TPU:8, one launch (start us, length us, event | category | flops | bytes accessed | tf_op | source)
XLA Modules:
  0.0 82.5 jit_solution(14166866723723916255)
XLA Ops:
  0.6 79.7 %hyena_backward.1 = (bf16[128,1024]{1,0:T(8,128)(2,1)}, bf16[128,1024]{1,0:T(8,128)(2,1)}, bf16[128,1024]{1,0:T(8,128)(2,1)}, bf16[256,1024]{1,0:T(8,128)(2,1)}) custom-call(bf16[128,1024]{1,0:T(8,128)(2,1)} %q_ref.1, bf16[128,1024]{1,0:T(8,128)(2,1)} %k_ref.1, bf16[128,1024]{1,0:T(8,128)(2,1)} %v_ref.1, bf16[128,1024]{1,0:T(8,128)(2,1)} %g_ref.1, ...), custom_call_target="tpu_custom_call" | custom-call | tf_op jit(solution)/shard_map/hyena_backward/pallas_call | solution.py:543
  80.4 2.1 %copy_out.1 = (bf16[128,1024]{1,0:T(8,128)(2,1)}, bf16[128,1024]{1,0:T(8,128)(2,1)}, bf16[128,1024]{1,0:T(8,128)(2,1)}, bf16[256,1024]{1,0:T(8,128)(2,1)}) custom-call(bf16[128,1024]{1,0:T(8,128)(2,1)} %get-tuple-element.8.refs_0_, bf16[128,1024]{1,0:T(8,128)(2,1)} %get-tuple-element.9.refs_1_, bf16[128,1024]{1,0:T(8,128)(2,1)} %get-tuple-element.10.refs_2_, ...), custom_call_target="tpu_custom_call" | custom-call | tf_op jit(solution)/shard_map/copy_out/pallas_call | solution.py:590

commit v3 on v2

--- a/solution.py
+++ b/solution.py
@@ -79,7 +79,7 @@
     qg_ref, cg_ref, gg_ref, wt_ref,
     prod, halo, og, wg, mr, tf, tb, base, rates_all, weights_all, coef_a, coef_e, carry, back, decay,
     conv, mixed, long_out, part, ends, ends_all, starts, starts_all, state,
-    rs_out, rs_in, gall, delta, ogt, x_out, x_in,
+    rs_out, rs_in, gall, delta, ogt, x_far_out, x_far_in, x_near_out, x_near_in, wt_sum,
     a2_send, a2_recv, loc, halo_send, halo_recv, w_send, w_recv, y_send, y_recv, sib_send, sib_recv,
     st_send, st_recv, rs_send, rs_recv, ag_send, ag_recv, x_send, x_recv,
 ):
@@ -283,53 +283,45 @@
         gall[c, :, lanes] = (g_ref[:, lanes].astype(F32) * total).astype(BF16)
         return carried
 
-    def ag_block(half, way, step, ahead):
-        rows = pl.ds(0, ROWS) if step < 3 else pl.ds(way * 64, 64)
-        return gall.at[ctx(-steps[way] * (step + ahead)), rows, halves[half]]
-
-    def ag_copy(half, way, step, ahead=0):
-        block = ag_block(half, way, step, ahead)
-        return remote(
-            block, block, ag_send.at[half, way, step], ag_recv.at[half, way, step], ctx=ctx(steps[way])
+    def rows_of(sub):
+        return pl.ds(sub * 64, 64)
+
+    def ag_copy(half, way, step, sub, ahead=0):
+        block = gall.at[ctx(-steps[way] * (step + ahead)), rows_of(sub), halves[half]]
+        return remote(
+            block, block, ag_send.at[half, way, step, sub], ag_recv.at[half, way, step, sub], ctx=ctx(steps[way])
         )
 
     def gather(half, step):
-        for way in range(2):
-            if step > 0:
-                ag_copy(half, way, step - 1, 1).wait_recv()
-            if step < 4:
-                ag_copy(half, way, step).start()
-
-    def rs_rows(way, step):
-        return pl.ds(way * 64, 64) if step == 0 else pl.ds(0, ROWS)
-
-    def rs_copy(half, way, step):
-        rows = rs_rows(way, step)
+        for sub in range(2):
+            for way in range(2):
+                if step > 0 and (step < 4 or sub == way):
+                    ag_copy(half, way, step - 1, sub, 1).wait_recv()
+                if step < 3 or (step == 3 and sub == way):
+                    ag_copy(half, way, step, sub).start()
+
+    def rs_copy(half, way, step, sub):
+        rows = rows_of(sub)
         return remote(
             rs_out.at[half, way, step, rows, :], rs_in.at[half, way, step, rows, :],
-            rs_send.at[half, way, step], rs_recv.at[half, way, step], ctx=ctx(steps[way]),
+            rs_send.at[half, way, step, sub], rs_recv.at[half, way, step, sub], ctx=ctx(steps[way]),
         )
 
     def reduce(half, step):
         lanes = halves[half]
-        for way in range(2):
-            if step > 0:
-                rs_copy(half, way, step - 1).wait_recv()
-            if step == 4:
-                continue
-            target = ctx(steps[way] * (4 - step))
-            if step < 2:
-                rows, rest = rs_rows(way, 0), rs_rows(1 - way, 0)
-                total = part[target, rows, lanes]
-                if step == 1:
-                    total = total + rs_in[half, way, 0, rows, :].astype(F32)
-                    rs_out[half, way, 1, rest, :] = part[target, rest, lanes].astype(BF16)
+        for sub in range(2):
+            rows = rows_of(sub)
+            for way in range(2):
+                arrives = step > 1 or (step == 1 and sub == way)
+                if arrives:
+                    rs_copy(half, way, step - 1, sub).wait_recv()
+                if step == 4 or (step == 0 and sub != way):
+                    continue
+                total = part[ctx(steps[way] * (4 - step)), rows, lanes]
+                if arrives:
+                    total = total + rs_in[half, way, step - 1, rows, :].astype(F32)
                 rs_out[half, way, step, rows, :] = total.astype(BF16)
-            else:
-                rs_out[half, way, step] = (
-                    part[target, :, lanes] + rs_in[half, way, step - 1].astype(F32)
-                ).astype(BF16)
-            rs_copy(half, way, step).start()
+                rs_copy(half, way, step, sub).start()
 
     def project(n, carried):
         channels = pl.ds(pl.multiple_of(n * FEATS, FEATS), FEATS)
@@ -383,21 +375,42 @@
         rows = pl.ds(pl.multiple_of(owner * FEATS, FEATS), FEATS)
         return dot(ogt[rows, :], gall[:, :, halves[half]].reshape(N_CTX * ROWS, HALF))
 
-    def x_copy(half, s):
-        return remote(
-            x_out.at[half, s - 1], x_in.at[half, s - 1], x_send.at[half, s], x_recv.at[half, s], dp=dp(s)
-        )
-
-    def weight_send(half):
-        for s in (2, 1, 3):
-            x_out[half, s - 1] = weight_part(half, dp(s)).astype(BF16)
-            x_copy(half, s).start()
+    def x_far_copy(half, way):
+        return remote(
+            x_far_out.at[half, way], x_far_in.at[half, way],
+            x_send.at[half, way], x_recv.at[half, way], dp=dp(steps[way]),
+        )
+
+    def x_near_copy(half, way):
+        return remote(
+            x_near_out.at[half, way], x_near_in.at[half, way],
+            x_send.at[half, 2 + way], x_recv.at[half, 2 + way], dp=dp(steps[way]),
+        )
+
+    def weight_far(half):
+        opposite = weight_part(half, dp(2))
+        for way in range(2):
+            x_far_out[half, way] = opposite[way * 128 : (way + 1) * 128].astype(BF16)
+            x_far_copy(half, way).start()
+
+    def weight_near(half):
+        for way in range(2):
+            near = weight_part(half, dp(steps[way]))
+            mine = slice(way * 128, way * 128 + 128)
+            other = slice((1 - way) * 128, (1 - way) * 128 + 128)
+            x_near_out[half, way, other, :] = near[other].astype(BF16)
+            x_far_copy(half, way).wait_recv()
+            x_near_out[half, way, mine, :] = (near[mine] + x_far_in[half, way].astype(F32)).astype(BF16)
+            x_near_copy(half, way).start()
+
+    def weight_own(half):
+        wt_sum[half] = weight_part(half, d)
 
     def weight_finish(half):
-        own = weight_part(half, d)
-        for s in range(1, N_DP):
-            x_copy(half, s).wait_recv()
-            own = own + x_in[half, s - 1].astype(F32)
+        own = wt_sum[half]
+        for way in range(2):
+            x_near_copy(half, way).wait_recv()
+            own = own + x_near_in[half, way].astype(F32)
         wt_ref[:, half * HALF : (half + 1) * HALF] = own.astype(BF16)
 
     def strips(owner):
@@ -471,25 +484,29 @@
     lax.fori_loop(0, N_CTX, transpose_rows, 0)
     reduce(1, 1)
     gather(0, 4)
-    weight_send(0)
+    weight_far(0)
     reduce(0, 2)
     gather(1, 4)
     reduce(1, 2)
-    weight_send(1)
+    weight_far(1)
+    weight_near(0)
     reduce(0, 3)
     reduce(1, 3)
     reduce(0, 4)
     begin_back_of(0)
+    weight_near(1)
     each(0, local_back)
-    weight_finish(0)
     reduce(1, 4)
     begin_back_of(1)
     each(1, local_back)
     gather_states(0, back_in, starts_all, range(N_CTX - 1, 0, -1), lambda source: source > c)
     each(0, finish_back)
-    weight_finish(1)
+    weight_own(0)
+    weight_own(1)
+    weight_finish(0)
     gather_states(1, back_in, starts_all, range(N_CTX - 1, 0, -1), lambda source: source > c)
     each(1, finish_back)
+    weight_finish(1)
 
     for s in range(1, N_CTX):
         for j in range(N_DP):
@@ -512,11 +529,15 @@
         halo_copy(half).wait_send()
         for s in range(1, N_DP):
             w_copy(half, s).wait_send()
-            x_copy(half, s).wait_send()
         for way in range(2):
+            x_far_copy(half, way).wait_send()
+            x_near_copy(half, way).wait_send()
             for step in range(4):
-                rs_copy(half, way, step).wait_send()
-                ag_copy(half, way, step).wait_send()
+                for sub in range(2):
+                    if step > 0 or sub == way:
+                        rs_copy(half, way, step, sub).wait_send()
+                    if step < 3 or sub == way:
+                        ag_copy(half, way, step, sub).wait_send()
 
 
 def copy_out(*refs):
@@ -575,12 +596,15 @@
             pltpu.VMEM((N_CTX, ROWS, WIDTH), BF16),
             pltpu.VMEM((ROWS, WIDTH), F32),
             pltpu.VMEM((WIDTH, N_CTX * ROWS), BF16),
-            pltpu.VMEM((2, N_DP - 1, FEATS, HALF), BF16),
-            pltpu.VMEM((2, N_DP - 1, FEATS, HALF), BF16),
+            pltpu.VMEM((2, 2, 128, HALF), BF16),
+            pltpu.VMEM((2, 2, 128, HALF), BF16),
+            pltpu.VMEM((2, 2, FEATS, HALF), BF16),
+            pltpu.VMEM((2, 2, FEATS, HALF), BF16),
+            pltpu.VMEM((2, FEATS, HALF), F32),
             dma((N_CTX, N_DP)), dma((N_CTX, N_DP)), dma((N_DP + 1,)), dma((2,)), dma((2,)),
             dma((2, N_DP)), dma((2, N_DP)), dma((N_Y,)), dma((N_Y,)), dma((N_Y,)), dma((N_Y,)),
-            dma((2, 2, N_CTX)), dma((2, 2, N_CTX)), dma((2, 2, 4)), dma((2, 2, 4)),
-            dma((2, 2, 4)), dma((2, 2, 4)), dma((2, N_DP)), dma((2, N_DP)),
+            dma((2, 2, N_CTX)), dma((2, 2, N_CTX)), dma((2, 2, 4, 2)), dma((2, 2, 4, 2)),
+            dma((2, 2, 4, 2)), dma((2, 2, 4, 2)), dma((2, N_DP)), dma((2, N_DP)),
         ],
         compiler_params=pltpu.CompilerParams(
             collective_id=0, has_side_effects=True, vmem_limit_bytes=56 * 1024 * 1024

time: 83.2 us -> 82.7 us (level)
  no operation moved by 1% of the time
where the time goes in v3:
time: 82.7 us; the launch traced here: 82.3 us
  Pallas kernels  81.6 us (99%)
    pallas_call x1, Pallas kernels, on_device(): pl.pallas_call(kernel, out_shape=outs, in_specs=[vmem, vmem, vmem, vmem,...  79.5 us
    pallas_call x1, Pallas kernels, on_device(): pl.pallas_call(copy_out, out_shape=outs, in_specs=[hbm] * 4, out_specs=(h...  2.15 us

profile of v3, /device:TPU:8, one launch (start us, length us, event | category | flops | bytes accessed | tf_op | source)
XLA Modules:
  0.0 82.3 jit_solution(14251887164770950419)
XLA Ops:
  0.6 79.5 %hyena_backward.1 = (bf16[128,1024]{1,0:T(8,128)(2,1)}, bf16[128,1024]{1,0:T(8,128)(2,1)}, bf16[128,1024]{1,0:T(8,128)(2,1)}, bf16[256,1024]{1,0:T(8,128)(2,1)}) custom-call(bf16[128,1024]{1,0:T(8,128)(2,1)} %q_ref.1, bf16[128,1024]{1,0:T(8,128)(2,1)} %k_ref.1, bf16[128,1024]{1,0:T(8,128)(2,1)} %v_ref.1, bf16[128,1024]{1,0:T(8,128)(2,1)} %g_ref.1, ...), custom_call_target="tpu_custom_call" | custom-call | tf_op jit(solution)/shard_map/hyena_backward/pallas_call | solution.py:564
  80.1 2.1 %copy_out.1 = (bf16[128,1024]{1,0:T(8,128)(2,1)}, bf16[128,1024]{1,0:T(8,128)(2,1)}, bf16[128,1024]{1,0:T(8,128)(2,1)}, bf16[256,1024]{1,0:T(8,128)(2,1)}) custom-call(bf16[128,1024]{1,0:T(8,128)(2,1)} %get-tuple-element.8.refs_0_, bf16[128,1024]{1,0:T(8,128)(2,1)} %get-tuple-element.9.refs_1_, bf16[128,1024]{1,0:T(8,128)(2,1)} %get-tuple-element.10.refs_2_, ...), custom_call_target="tpu_custom_call" | custom-call | tf_op jit(solution)/shard_map/copy_out/pallas_call | solution.py:614

commit v4 on v3

--- a/solution.py
+++ b/solution.py
@@ -540,20 +540,6 @@
                         ag_copy(half, way, step, sub).wait_send()
 
 
-def copy_out(*refs):
-    count = len(refs) // 3
-    results, outs, held, sems = refs[:count], refs[count : 2 * count], refs[2 * count : -1], refs[-1]
-    arrive = [pltpu.make_async_copy(results[i], held[i], sems.at[0, i]) for i in range(count)]
-    leave = [pltpu.make_async_copy(held[i], outs[i], sems.at[1, i]) for i in range(count)]
-    for copy in arrive:
-        copy.start()
-    for i in range(count):
-        arrive[i].wait()
-        leave[i].start()
-    for copy in leave:
-        copy.wait()
-
-
 def on_device(query, key_in, value_in, gate, out_grad, proj_weight, mr_filter, lr_rate, lr_residue):
     vmem = pl.BlockSpec(memory_space=pltpu.VMEM)
     hbm = pl.BlockSpec(memory_space=pl.ANY)
@@ -561,9 +547,9 @@
     outs = (act, act, act, jax.ShapeDtypeStruct((FEATS, WIDTH), BF16))
     dma = pltpu.SemaphoreType.DMA
     stacked = (BLOCKS, 8 * ROWS, LANES)
-    results = pl.pallas_call(
+    return pl.pallas_call(
         kernel,
-        out_shape=outs,
+        out_shape=tuple(pltpu.VMEM(out.shape, out.dtype) for out in outs),
         in_specs=[vmem, vmem, vmem, vmem, hbm, hbm, vmem, vmem, vmem],
         out_specs=(vmem, vmem, vmem, vmem),
         scratch_shapes=[
@@ -611,14 +597,6 @@
         ),
         name="hyena_backward",
     )(query, key_in, value_in, gate, out_grad, proj_weight, mr_filter, lr_rate.T, lr_residue.T)
-    return pl.pallas_call(
-        copy_out,
-        out_shape=outs,
-        in_specs=[hbm] * 4,
-        out_specs=(hbm,) * 4,
-        scratch_shapes=[pltpu.VMEM(out.shape, out.dtype) for out in outs] + [dma((2, 4))],
-        name="copy_out",
-    )(*results)
 
 
 def solution(mesh):

time: 82.7 us -> 82.4 us (level)
  Pallas kernels: 81.6 us -> 78.4 us
  local copies, waits for them, and re-layouts: 0 us -> 2.9 us
    pallas_call x2 -> x1, Pallas kernels: 81.6 us -> 78.4 us  [on_device(): pl.pallas_call(kernel, out_shape=tuple((pltpu.VMEM(out.shape, out.dtype)...]
    unnamed x0 -> x4, local copies, waits for them, and re-layouts: none -> 2.9 us
where the time goes in v4:
time: 82.4 us; the launch traced here: 81.9 us
  Pallas kernels  78.4 us (95%)
  local copies, waits for them, and re-layouts  2.9 us (4%)
    pallas_call x1, Pallas kernels, on_device(): pl.pallas_call(kernel, out_shape=tuple((pltpu.VMEM(out.shape, out.dtype)...  78.4 us
    unnamed x4, local copies, waits for them, and re-layouts  2.9 us

profile of v4, /device:TPU:8, one launch (start us, length us, event | category | flops | bytes accessed | tf_op | source)
XLA Modules:
  0.0 81.9 jit_solution(17703717475619362923)
XLA Ops:
  0.6 78.4 %hyena_backward.1 = (bf16[128,1024]{1,0:T(8,128)(2,1)S(1)}, bf16[128,1024]{1,0:T(8,128)(2,1)S(1)}, bf16[128,1024]{1,0:T(8,128)(2,1)S(1)}, bf16[256,1024]{1,0:T(8,128)(2,1)S(1)}) custom-call(bf16[128,1024]{1,0:T(8,128)(2,1)} %q_ref.1, bf16[128,1024]{1,0:T(8,128)(2,1)} %k_ref.1, bf16[128,1024]{1,0:T(8,128)(2,1)} %v_ref.1, bf16[128,1024]{1,0:T(8,128)(2,1)} %g_ref.1, ...), custom_call_target="tpu_custom_call" | custom-call | tf_op jit(solution)/shard_map/hyena_backward/pallas_call | solution.py:550
  79.0 0.7 copy.17
  79.7 0.7 copy.18
  80.4 0.7 copy.19
  81.1 0.8 copy.20
